TPU v7x, 32 devices: a whole 2x2x4 slice. The times are simulated.
32 devices in a mesh: tx: 8 (over z, core), ty: 4 (over y, x).
Axes of the slice: x: 2, y: 2, z: 4, core: 2. Of those that a mesh axis runs over, the one named last changes fastest.
Arguments:
- camera: int32 [64, 128], P('ty', 'tx'), may hold values from 0 to 99
- ray_mask: int32 [64, 128], P('ty', 'tx'), may hold values 0 or 1
- ray_direction: float32 [3, 64, 128], P(None, 'ty', 'tx'), may hold values from -1 to 1
- anchors: float32 [3, 100], replicated, may hold values from -1 to 1
- target: float32 [3, 64, 128], P(None, 'ty', 'tx'), may hold values from 0 to 1
- fine_levels: int32 [128, 64, 128], P(None, 'ty', 'tx'), may hold values from 0 to 1023, as said below
- density_bins: int32 [128, 64, 128], P(None, 'ty', 'tx'), may hold values from 0 to 63
- owners: int32 [5, 2], replicated, may hold values from 0 to 31
- encoder: float32 [32, 2, 256, 63], P(('tx', 'ty')), may hold values from -0.75 to 0.75
- middle: float32 [32, 2, 256, 256], P(('tx', 'ty')), may hold values from -0.375 to 0.375
- viewer: float32 [32, 2, 128, 283], P(('tx', 'ty')), may hold values from -0.375 to 0.375
- colour: float32 [32, 2, 3, 128], P(('tx', 'ty')), may hold values from -0.5 to 0.5
- scalars: float32 [32, 2, 900], P(('tx', 'ty')), may hold values from -0.375 to 0.375
- moment_encoder: float32 [32, 2, 256, 63], P(('tx', 'ty')), may hold values from -0.00061035156 to 0.00061035156
- moment_middle: float32 [32, 2, 256, 256], P(('tx', 'ty')), may hold values from -0.00061035156 to 0.00061035156
- moment_viewer: float32 [32, 2, 128, 283], P(('tx', 'ty')), may hold values from -0.00061035156 to 0.00061035156
- moment_colour: float32 [32, 2, 3, 128], P(('tx', 'ty')), may hold values from -0.00061035156 to 0.00061035156
- moment_scalars: float32 [32, 2, 900], P(('tx', 'ty')), may hold values from -0.00061035156 to 0.00061035156
- square_encoder: float32 [32, 2, 256, 63], P(('tx', 'ty')), may hold values from 9.536744e-10 to 3.8146974e-09
- square_middle: float32 [32, 2, 256, 256], P(('tx', 'ty')), may hold values from 9.536744e-10 to 3.8146974e-09
- square_viewer: float32 [32, 2, 128, 283], P(('tx', 'ty')), may hold values from 9.536744e-10 to 3.8146974e-09
- square_colour: float32 [32, 2, 3, 128], P(('tx', 'ty')), may hold values from 9.536744e-10 to 3.8146974e-09
- square_scalars: float32 [32, 2, 900], P(('tx', 'ty')), may hold values from 9.536744e-10 to 3.8146974e-09
Outputs:
- total_loss: float32 [], replicated
- density_histogram: float32 [64], replicated
- next_encoder: float32 [32, 2, 256, 63], P(('tx', 'ty'))
- next_middle: float32 [32, 2, 256, 256], P(('tx', 'ty'))
- next_viewer: float32 [32, 2, 128, 283], P(('tx', 'ty'))
- next_colour: float32 [32, 2, 3, 128], P(('tx', 'ty'))
- next_scalars: float32 [32, 2, 900], P(('tx', 'ty'))
- encoder_moment: float32 [32, 2, 256, 63], P(('tx', 'ty'))
- middle_moment: float32 [32, 2, 256, 256], P(('tx', 'ty'))
- viewer_moment: float32 [32, 2, 128, 283], P(('tx', 'ty'))
- colour_moment: float32 [32, 2, 3, 128], P(('tx', 'ty'))
- scalars_moment: float32 [32, 2, 900], P(('tx', 'ty'))
- encoder_square: float32 [32, 2, 256, 63], P(('tx', 'ty'))
- middle_square: float32 [32, 2, 256, 256], P(('tx', 'ty'))
- viewer_square: float32 [32, 2, 128, 283], P(('tx', 'ty'))
- colour_square: float32 [32, 2, 3, 128], P(('tx', 'ty'))
- scalars_square: float32 [32, 2, 900], P(('tx', 'ty'))
Inputs may be any that keep to these rules, and one draw needn't show every extreme that they name: `fine_levels`: each ray's 128 fine levels never fall along the first dimension.
All inputs are finite; a program needn't handle non-finite values. No bound on the sum of `ray_mask` on one device may be relied on, other than what follows from the above.
Results may differ from a plain program's by a relative error of at most 0.0003.
The roundings to bfloat16 on the way count: a program that leaves them out, or rounds other values in their place, can miss the bound.
Values may be sent and summed in bfloat16 or wider, within the bound.
A program may use at most 64 MiB of HBM per device.

v0:
```python
import math

import jax
import jax.numpy as jnp
from jax import lax
from jax.sharding import PartitionSpec as P

LPOS = 10
LDIR = 4
SC = 64
NT = 1024
NHIST = 64


near_plane = 2.0
far_plane = 6.0
shrink = 0.125
smooth_weight = 0.1
entropy_weight = 0.1
beta_first = 0.9
beta_second = 0.999
adam_epsilon = 1e-08
decay_rate = 0.01
learn_rate = 0.05
step_count = 10
ray_block = 32


def passed_along(block, axis, distance):
    devices = range(lax.axis_size(axis))
    route = [(i - distance, i) for i in devices if i - distance in devices]
    return lax.ppermute(block, axis, route)


def encode(points, levels):
    scales = 2.0 ** jnp.arange(levels, dtype=jnp.float32) * math.pi
    angles = points[None] * scales.reshape((levels,) + (1,) * points.ndim)
    wavesets = jnp.stack([jnp.sin(angles), jnp.cos(angles)], axis=1)
    return jnp.concatenate([points, wavesets.reshape((6 * levels,) + points.shape[1:])], axis=0)


def split_scalars(scalars, hidden, view_width):
    offset = 3 * hidden + 1
    return (
        scalars[:hidden],
        scalars[hidden : 2 * hidden],
        scalars[2 * hidden : 3 * hidden],
        scalars[3 * hidden],
        scalars[offset : offset + view_width],
        scalars[offset + view_width :],
    )


def contract(former, latter):
    return lax.dot_general(
        former, latter, (((1,), (1,)), ((), ())), preferred_element_type=jnp.float32
    )


def transposed(weight, gradient):
    return lax.dot_general(
        weight, gradient, (((0,), (0,)), ((), ())), preferred_element_type=jnp.float32
    )


def to_blocks(values, pieces):
    ray_width = values.shape[-1] // pieces
    shaped = values.reshape(values.shape[:-1] + (pieces, ray_width))
    return jnp.moveaxis(shaped, -2, 0)


def from_blocks(values):
    merged = jnp.moveaxis(values, 0, -2)
    return merged.reshape(merged.shape[:-2] + (merged.shape[-2] * merged.shape[-1],))


def composite(density, colours, depths):
    spacing = jnp.concatenate([depths[1:] - depths[:-1], far_plane - depths[-1:]], 0)
    optical = density * spacing
    before = jnp.cumsum(optical, 0) - optical
    weights = jnp.exp(-before) * (1.0 - jnp.exp(-optical))
    return (
        spacing,
        optical,
        before,
        weights,
        jnp.sum(weights[None] * colours, 1),
        jnp.sum(weights * depths, 0),
        jnp.sum(weights, 0),
    )


def composite_back(colours, depths, parts, colour_seed, depth_seed, opacity_seed):
    spacing, optical, before, weights = parts[:4]
    weight_grad = (
        jnp.sum(colour_seed[:, None, :] * colours, 0)
        + depth_seed[None] * depths
        + opacity_seed[None]
    )
    weighted = weight_grad * weights
    later = jnp.cumsum(weighted[::-1], 0)[::-1] - weighted
    optical_grad = weight_grad * jnp.exp(-(before + optical)) - later
    return (optical_grad * spacing, weights[None] * colour_seed[:, None, :])


def field_forward(params, encoded, view_code, samples):
    encoder, middle, viewer, colour, scalars = params
    hidden = middle.shape[0]
    view_width = viewer.shape[0]
    ray_width = view_code.shape[1]
    bias_one, bias_two, sigma_row, sigma_bias, view_bias, colour_bias = split_scalars(
        scalars, hidden, view_width
    )
    pre_one = (
        jnp.dot(encoder, encoded, preferred_element_type=jnp.float32)
        + bias_one.astype(jnp.float32)[:, None]
    )
    hidden_one = jax.nn.relu(pre_one).astype(jnp.bfloat16)
    pre_two = (
        jnp.dot(middle, hidden_one, preferred_element_type=jnp.float32)
        + bias_two.astype(jnp.float32)[:, None]
    )
    hidden_two = jax.nn.relu(pre_two).astype(jnp.bfloat16)
    pre_sigma = jnp.dot(sigma_row[None], hidden_two, preferred_element_type=jnp.float32)[
        0
    ] + sigma_bias.astype(jnp.float32)
    per_ray = jnp.dot(viewer[:, hidden:], view_code, preferred_element_type=jnp.float32)
    pre_view = jnp.dot(viewer[:, :hidden], hidden_two, preferred_element_type=jnp.float32).reshape(
        view_width, samples, ray_width
    )
    pre_view = pre_view + per_ray[:, None, :] + view_bias.astype(jnp.float32)[:, None, None]
    view_hidden = jax.nn.relu(pre_view.reshape(view_width, samples * ray_width)).astype(
        jnp.bfloat16
    )
    pre_colour = (
        jnp.dot(colour, view_hidden, preferred_element_type=jnp.float32)
        + colour_bias.astype(jnp.float32)[:, None]
    )
    return (
        hidden_one,
        hidden_two,
        view_hidden,
        pre_sigma,
        jax.nn.softplus(pre_sigma),
        jax.nn.sigmoid(pre_colour),
    )


def field_backward(params, encoded, view_code, samples, kept_values, density_grad, colour_grad):
    encoder, middle, viewer, colour, scalars = params
    hidden = middle.shape[0]
    view_width = viewer.shape[0]
    ray_width = view_code.shape[1]
    hidden_one, hidden_two, view_hidden, pre_sigma, density, colours = kept_values
    gate_sigma = (density_grad * jax.nn.sigmoid(pre_sigma)).astype(jnp.bfloat16)
    gate_colour = (colour_grad * colours * (1.0 - colours)).astype(jnp.bfloat16)
    grad_view = transposed(colour, gate_colour)
    gate_view = jnp.where(view_hidden > 0, grad_view, 0.0).astype(jnp.bfloat16)
    grad_colour = contract(gate_colour, view_hidden)
    ray_sums = jnp.sum(gate_view.astype(jnp.float32).reshape(view_width, samples, ray_width), 1)
    grad_viewer = jnp.concatenate(
        [
            contract(gate_view, hidden_two),
            jnp.dot(ray_sums, view_code.astype(jnp.float32).T, precision=lax.Precision.HIGHEST),
        ],
        1,
    )
    sigma_row = scalars[2 * hidden : 3 * hidden].astype(jnp.float32)
    grad_two = (
        transposed(viewer[:, :hidden], gate_view)
        + sigma_row[:, None] * gate_sigma.astype(jnp.float32)[None]
    )
    gate_two = jnp.where(hidden_two > 0, grad_two, 0.0).astype(jnp.bfloat16)
    grad_middle = contract(gate_two, hidden_one)
    grad_one = transposed(middle, gate_two)
    gate_one = jnp.where(hidden_one > 0, grad_one, 0.0).astype(jnp.bfloat16)
    grad_encoder = contract(gate_one, encoded)
    grad_scalars = jnp.concatenate(
        [
            jnp.sum(gate_one.astype(jnp.float32), 1),
            jnp.sum(gate_two.astype(jnp.float32), 1),
            contract(gate_sigma[None], hidden_two)[0],
            jnp.sum(gate_sigma.astype(jnp.float32))[None],
            jnp.sum(ray_sums, 1),
            jnp.sum(gate_colour.astype(jnp.float32), 1),
        ]
    )
    return (grad_encoder, grad_middle, grad_viewer, grad_colour, grad_scalars)


def render_piece(params, anchor_piece, direction_piece, view_code, depths):
    samples, ray_width = depths.shape
    points = (anchor_piece[:, None, :] + depths[None] * direction_piece[:, None, :]) * shrink
    encoded = encode(points, LPOS).astype(jnp.bfloat16).reshape(-1, samples * ray_width)
    kept_values = field_forward(params, encoded, view_code, samples)
    density = kept_values[4].reshape(samples, ray_width)
    colours = kept_values[5].reshape(3, samples, ray_width)
    return (encoded, kept_values, density, colours, composite(density, colours, depths))


def adamw_update(weight, moment, square, gradient):
    moment_next = beta_first * moment + (1.0 - beta_first) * gradient
    square_next = beta_second * square + (1.0 - beta_second) * gradient * gradient
    first_hat = moment_next / (1.0 - beta_first**step_count)
    second_hat = square_next / (1.0 - beta_second**step_count)
    weight_next = weight - learn_rate * (
        first_hat / (jnp.sqrt(second_hat) + adam_epsilon) + decay_rate * weight
    )
    return (weight_next, moment_next, square_next)


def per_device(
    camera,
    ray_mask,
    ray_direction,
    anchors,
    target,
    fine_levels,
    density_bins,
    owners,
    encoder,
    middle,
    viewer,
    colour,
    scalars,
    moment_encoder,
    moment_middle,
    moment_viewer,
    moment_colour,
    moment_scalars,
    square_encoder,
    square_middle,
    square_viewer,
    square_colour,
    square_scalars,
):
    masters = (encoder[0], middle[0], viewer[0], colour[0], scalars[0])
    moments = (
        moment_encoder[0],
        moment_middle[0],
        moment_viewer[0],
        moment_colour[0],
        moment_scalars[0],
    )
    squares = (
        square_encoder[0],
        square_middle[0],
        square_viewer[0],
        square_colour[0],
        square_scalars[0],
    )
    tile_rows, tile_cols = camera.shape
    ray_count = tile_rows * tile_cols
    cameras = anchors.shape[1]
    samples_fine = fine_levels.shape[0]
    camera_flat = camera.reshape(ray_count)
    mask_flat = ray_mask.reshape(ray_count).astype(jnp.float32)
    camera_picks = (camera_flat[None] == jnp.arange(cameras)[:, None]).astype(jnp.float32)
    camera_count = jnp.sum(camera_picks * mask_flat[None], 1)
    mask_total = jnp.sum(mask_flat)
    device = lax.axis_index(("tx", "ty"))

    def owned_shape(group_index):
        return (2,) + (1,) * (masters[group_index].ndim - 1)

    owned_parts = [
        jnp.where(
            (owners[group_index] == device).reshape(owned_shape(group_index)),
            masters[group_index].astype(jnp.bfloat16).astype(jnp.float32),
            0.0,
        )
        for group_index in range(5)
    ]
    summed = lax.psum(
        (
            owned_parts[0],
            owned_parts[1],
            owned_parts[2],
            owned_parts[3],
            owned_parts[4],
            camera_count,
            mask_total,
        ),
        ("tx", "ty"),
    )
    lowered = [summed[group_index].astype(jnp.bfloat16) for group_index in range(5)]
    camera_count = summed[5]
    mask_total = summed[6]
    coarse_params = tuple((member[0] for member in lowered))
    fine_params = tuple((member[1] for member in lowered))
    direction = ray_direction.reshape(3, ray_count)
    anchor = jnp.dot(anchors, camera_picks, precision=lax.Precision.HIGHEST)
    coarse_line = (
        near_plane + (far_plane - near_plane) * (jnp.arange(SC, dtype=jnp.float32) + 0.5) / SC
    )
    coarse_depths = jnp.broadcast_to(coarse_line[:, None], (SC, ray_count))
    fine_depths = (
        near_plane
        + (far_plane - near_plane)
        * (fine_levels.reshape(samples_fine, ray_count).astype(jnp.float32) + 0.5)
        / NT
    )
    block_rays = min(ray_block, ray_count)
    pieces = ray_count // block_rays
    blocks = (
        to_blocks(anchor, pieces),
        to_blocks(direction, pieces),
        to_blocks(coarse_depths, pieces),
        to_blocks(fine_depths, pieces),
    )

    def forward_piece(inputs):
        anchor_piece, direction_piece, coarse_piece, fine_piece = inputs
        view_code = encode(direction_piece, LDIR).astype(jnp.bfloat16)
        coarse_state = render_piece(
            coarse_params, anchor_piece, direction_piece, view_code, coarse_piece
        )
        fine_state = render_piece(fine_params, anchor_piece, direction_piece, view_code, fine_piece)
        return (
            coarse_state[4][4],
            fine_state[4][4],
            fine_state[4][5],
            fine_state[4][6],
            fine_state[2],
        )

    results = lax.map(forward_piece, blocks)
    colour_coarse, colour_fine, depth_fine, opacity_fine, density_fine = tuple(
        (from_blocks(member) for member in results)
    )
    mask_floor = jnp.maximum(mask_total, 1.0)
    inverse = 1.0 / jnp.maximum(camera_count, 1.0)
    ray_weight = jnp.sum(camera_picks * inverse[:, None], 0) * mask_flat / cameras
    target_flat = target.reshape(3, ray_count)
    miss_coarse = colour_coarse - target_flat
    miss_fine = colour_fine - target_flat
    loss_part = jnp.sum(ray_weight * jnp.sum(miss_coarse * miss_coarse, 0)) + jnp.sum(
        ray_weight * jnp.sum(miss_fine * miss_fine, 0)
    )
    grid_values = jnp.concatenate([colour_fine, depth_fine[None]], 0).reshape(
        4, tile_rows, tile_cols
    )
    grid_mask = mask_flat.reshape(tile_rows, tile_cols)
    right_values, right_mask = passed_along((grid_values[:, :, 0], grid_mask[:, 0]), "tx", -1)
    lower_values, lower_mask = passed_along((grid_values[:, 0, :], grid_mask[0, :]), "ty", -1)
    wide_values = jnp.concatenate([grid_values, right_values[:, :, None]], 2)
    wide_mask = jnp.concatenate([grid_mask, right_mask[:, None]], 1)
    tall_values = jnp.concatenate([grid_values, lower_values[:, None, :]], 1)
    tall_mask = jnp.concatenate([grid_mask, lower_mask[None, :]], 0)
    across = wide_values[:, :, 1:] - wide_values[:, :, :-1]
    across_pair = wide_mask[:, 1:] * wide_mask[:, :-1]
    downward = tall_values[:, 1:] - tall_values[:, :-1]
    down_pair = tall_mask[1:] * tall_mask[:-1]
    smooth_part = jnp.sum(across_pair[None] * across * across) + jnp.sum(
        down_pair[None] * downward * downward
    )
    opacity = 0.01 + 0.98 * opacity_fine
    entropy_part = -jnp.sum(
        mask_flat * (opacity * jnp.log(opacity) + (1.0 - opacity) * jnp.log(1.0 - opacity))
    )
    loss_part = (
        loss_part + (smooth_weight * smooth_part + entropy_weight * entropy_part) / mask_floor
    )
    bucket_rows = density_bins.reshape(samples_fine, ray_count)
    buckets = jnp.arange(NHIST)
    density_part = jnp.sum(
        jnp.where(
            bucket_rows[None] == buckets[:, None, None], (density_fine * mask_flat[None])[None], 0.0
        ),
        axis=(1, 2),
    )
    density_total = lax.psum(density_part, ("tx", "ty"))
    smooth_scale = smooth_weight / mask_floor
    grad_across = 2.0 * smooth_scale * across_pair[None] * across
    grad_down = 2.0 * smooth_scale * down_pair[None] * downward
    grad_wide = jnp.pad(grad_across, ((0, 0), (0, 0), (1, 0))) - jnp.pad(
        grad_across, ((0, 0), (0, 0), (0, 1))
    )
    grad_tall = jnp.pad(grad_down, ((0, 0), (1, 0), (0, 0))) - jnp.pad(
        grad_down, ((0, 0), (0, 1), (0, 0))
    )
    grad_grid = grad_wide[:, :, :tile_cols] + grad_tall[:, :tile_rows, :]
    back_right = passed_along(grad_wide[:, :, tile_cols], "tx", 1)
    back_lower = passed_along(grad_tall[:, tile_rows, :], "ty", 1)
    grad_grid = grad_grid.at[:, :, 0].add(back_right).at[:, 0, :].add(back_lower)
    grad_flat = grad_grid.reshape(4, ray_count)
    seed_coarse = 2.0 * ray_weight[None] * miss_coarse
    seed_fine = 2.0 * ray_weight[None] * miss_fine + grad_flat[:3]
    seed_depth = grad_flat[3]
    seed_opacity = (
        -(entropy_weight / mask_floor)
        * mask_flat
        * 0.98
        * (jnp.log(opacity) - jnp.log(1.0 - opacity))
    )
    back_inputs = blocks + (
        to_blocks(seed_coarse, pieces),
        to_blocks(seed_fine, pieces),
        to_blocks(seed_depth, pieces),
        to_blocks(seed_opacity, pieces),
    )

    def backward_piece(totals, inputs):
        (
            anchor_piece,
            direction_piece,
            coarse_piece,
            fine_piece,
            coarse_seed,
            fine_seed,
            depth_seed,
            opacity_seed,
        ) = inputs
        view_code = encode(direction_piece, LDIR).astype(jnp.bfloat16)
        zero_seed = jnp.zeros(coarse_piece.shape[1:], jnp.float32)
        net_plans = (
            (coarse_params, coarse_piece, coarse_seed, zero_seed, zero_seed),
            (fine_params, fine_piece, fine_seed, depth_seed, opacity_seed),
        )
        per_net = []
        for params, depths, colour_seed, depth_grad, opacity_grad in net_plans:
            encoded, kept_values, density, colours, parts = render_piece(
                params, anchor_piece, direction_piece, view_code, depths
            )
            density_grad, colour_grad = composite_back(
                colours, depths, parts, colour_seed, depth_grad, opacity_grad
            )
            per_net.append(
                field_backward(
                    params,
                    encoded,
                    view_code,
                    depths.shape[0],
                    kept_values,
                    density_grad.reshape(-1),
                    colour_grad.reshape(3, -1),
                )
            )
        updated = tuple(
            (
                total + jnp.stack([per_net[0][group_index], per_net[1][group_index]])
                for group_index, total in enumerate(totals)
            )
        )
        return (updated, None)

    initial = tuple((jnp.zeros(member.shape, jnp.float32) for member in lowered))
    totals = lax.scan(backward_piece, initial, back_inputs)[0]
    summed = lax.psum(
        (totals[0], totals[1], totals[2], totals[3], totals[4], loss_part), ("tx", "ty")
    )
    histogram = density_total / mask_floor
    next_list = []
    moment_list = []
    square_list = []
    for group_index in range(5):
        weight_next, moment_next, square_next = adamw_update(
            masters[group_index], moments[group_index], squares[group_index], summed[group_index]
        )
        owned_mask = (owners[group_index] == device).reshape(owned_shape(group_index))
        next_list.append(jnp.where(owned_mask, weight_next, masters[group_index])[None])
        moment_list.append(jnp.where(owned_mask, moment_next, moments[group_index])[None])
        square_list.append(jnp.where(owned_mask, square_next, squares[group_index])[None])
    return (
        summed[5],
        histogram,
        next_list[0],
        next_list[1],
        next_list[2],
        next_list[3],
        next_list[4],
        moment_list[0],
        moment_list[1],
        moment_list[2],
        moment_list[3],
        moment_list[4],
        square_list[0],
        square_list[1],
        square_list[2],
        square_list[3],
        square_list[4],
    )


def solution(mesh):
    in_specs = (
        P("ty", "tx"),
        P("ty", "tx"),
        P(None, "ty", "tx"),
        P(),
        P(None, "ty", "tx"),
        P(None, "ty", "tx"),
        P(None, "ty", "tx"),
        P(),
        P(("tx", "ty"), None, None, None),
        P(("tx", "ty"), None, None, None),
        P(("tx", "ty"), None, None, None),
        P(("tx", "ty"), None, None, None),
        P(("tx", "ty"), None, None),
        P(("tx", "ty"), None, None, None),
        P(("tx", "ty"), None, None, None),
        P(("tx", "ty"), None, None, None),
        P(("tx", "ty"), None, None, None),
        P(("tx", "ty"), None, None),
        P(("tx", "ty"), None, None, None),
        P(("tx", "ty"), None, None, None),
        P(("tx", "ty"), None, None, None),
        P(("tx", "ty"), None, None, None),
        P(("tx", "ty"), None, None),
    )
    out_specs = (
        P(),
        P(),
        P(("tx", "ty"), None, None, None),
        P(("tx", "ty"), None, None, None),
        P(("tx", "ty"), None, None, None),
        P(("tx", "ty"), None, None, None),
        P(("tx", "ty"), None, None),
        P(("tx", "ty"), None, None, None),
        P(("tx", "ty"), None, None, None),
        P(("tx", "ty"), None, None, None),
        P(("tx", "ty"), None, None, None),
        P(("tx", "ty"), None, None),
        P(("tx", "ty"), None, None, None),
        P(("tx", "ty"), None, None, None),
        P(("tx", "ty"), None, None, None),
        P(("tx", "ty"), None, None, None),
        P(("tx", "ty"), None, None),
    )
    return jax.shard_map(
        per_device, mesh=mesh, in_specs=in_specs, out_specs=out_specs, check_vma=False
    )
```

profile of v0, /device:TPU:0, one launch (start us, length us, event | category | flops | bytes accessed | tf_op | source)
XLA Modules:
  0.0 1293.4 jit_solution(6614407034433559449)
XLA Ops:
  20.8 55.6 %all-reduce.12 = (bf16[2,256,63]{1,2,0:T(8,128)(2,1)S(1)}, bf16[2,900]{1,0:T(2,128)(2,1)S(1)}, bf16[2,256,256]{2,1,0:T(8,128)(2,1)S(1)}, bf16[2,128,283]{1,2,0:T(8,128)(2,1)S(1)}, bf16[2,3,128]{2,0,1:T(2,128)(2,1)S(1)}) all-reduce(f32[2,256,63]{1,2,0:T(8,128)S(1)} %convert_select_fusion.2, ...), channel_id=1, replica_groups=mesh['tx'=8,'ty'=4] {'tx','ty'}, use_global_device_ids=true, to_apply=%region_4.5 | all-reduce | flops 238344 | bytes 1430064 | tf_op jit(solution)/shard_map/psum | solution.py:274
  81.5 309.7 %while.39 = (s32[]{:T(128)}, f32[8,3,32]{2,0,1:T(8,128)}, f32[8,3,32]{2,0,1:T(8,128)S(1)}, f32[8,32]{1,0:T(8,128)}, f32[8,32]{1,0:T(8,128)S(1)}, /*index=5*/f32[...) while((s32[]{:T(128)}, f32[8,3,32]{2,0,1:T(8,128)}, ...), condition=%wide.region_15.16_spmd, body=%wide.region_8.15_spmd.sunk | while | flops 1430527616 | bytes 23734316 | solution.py:327
  93.8 3.9 fusion.419
  107.1 3.1 concatenate.145
  132.5 3.9 fusion.419
  171.1 3.9 fusion.419
  209.8 3.9 fusion.419
  248.5 3.9 fusion.419
  287.1 3.9 fusion.419
  325.8 3.9 fusion.419
  364.4 3.9 fusion.419
  398.4 42.0 %all-reduce.5 = (f32[100]{0:T(128)S(1)}, f32[]{:T(128)}) all-reduce(f32[100]{0:T(128)S(1)} %select_reduce_fusion.2, f32[]{:T(128)} %get-tuple-element.652), channel_id=1, replica_groups=mesh['tx'=8,'ty'=4] {'tx','ty'}, use_global_device_ids=true, to_apply=%region_1.0 | all-reduce | flops 101 | bytes 808 | tf_op jit(solution)/shard_map/psum | solution.py:274
  448.5 4.2 collective-permute-start.5
  457.4 682.9 %while.40 = (s32[]{:T(128)}, f32[2,256,63]{1,2,0:T(8,128)}, f32[2,256,256]{2,1,0:T(8,128)}, f32[2,128,283]{2,1,0:T(8,128)}, f32[2,3,128]{2,1,0:T(4,128)}, /*inde...) while((s32[]{:T(128)}, f32[2,256,63]{1,2,0:T(8,128)}, ...), condition=%wide.region_47.48_spmd.clone, body=%wide.region_28.47_spmd.clone.sunk | while | flops 4086824704 | bytes 125729872 | solution.py:448
  490.6 3.9 fusion.498
  573.7 3.9 fusion.498
  657.4 3.9 fusion.498
  741.2 3.9 fusion.498
  825.0 3.9 fusion.498
  908.7 3.9 fusion.498
  992.5 3.9 fusion.498
  1076.2 3.9 fusion.498
  1145.6 41.1 %all-reduce.4 = (f32[]{:T(128)}, f32[64]{0:T(128)S(1)}, f32[2,3,128]{2,0,1:T(2,128)S(1)}, f32[2,900]{1,0:T(2,128)S(1)}) all-reduce(f32[]{:T(128)S(6)} %add.703, f32[64]{0:T(128)} %select_reduce_fusion, f32[2,3,128]{2,0,1:T(2,128)S(1)} %copy.239, f32[2,900]{1,0:T(2,128)} %get-tuple-element.282), channel_id=1, replica_groups=mesh['tx'=8,'ty'=4] {'tx','ty'}, use_global_device_ids=true, to_apply=%region_25.26 | all-reduce | flops 2633 | bytes 21064 | tf_op jit(solution)/shard_map/psum | solution.py:449
  1190.0 87.0 %all-reduce.11.cloned.1.call-done = (f32[2,256,63]{1,2,0:T(8,128)}, f32[2,256,256]{2,1,0:T(8,128)}, f32[2,128,283]{1,2,0:T(8,128)}) async-done(((f32[2,256,63]{1,2,0:T(8,128)}, f32[2,256,256]{2,1,0:T(8,128)}, f32[2,128,283]{1,2,0:T(8,128)}), (f32[2,256,63]{1,2,0:T(8,128)}, f32[2,256,256]{2,1,0:T(8,128)}, f32[2,128,283]{1,2,0:T(8,128)})) %all-reduce.11.cloned.1.call-update) | async-done | bytes 943120 | tf_op jit(solution)/shard_map/psum | solution.py:449
  (2490 shorter events, 935.3 us)
Async XLA Ops:
  7.2 1269.8 %all-reduce.11.cloned.1.call-start = ((), (), s32[]{:S(2)}) async-start(), calls=%async_computation | async-start | bytes 1900544 | tf_op jit(solution)/shard_map/psum | solution.py:449
  8.6 434.7 %collective-permute-start = (f32[16]{0:T(128)}, f32[16]{0:T(128)}, u32[]{:S(2)}, u32[]{:S(2)}) collective-permute-start(f32[16]{0:T(128)} %slice_reduce_fusion.1), channel_id=1, source_target_pairs={{4,0},{8,4},{12,8},{16,12},{20,16},{24,20},{28,24},{5,1},{9,5},{13... | collective-permute-start | bytes 200 | tf_op jit(solution)/shard_map/ppermute | solution.py:32
  10.4 433.7 %collective-permute-start.2 = (f32[16]{0:T(128)}, f32[16]{0:T(128)}, u32[]{:S(2)}, u32[]{:S(2)}) collective-permute-start(f32[16]{0:T(128)} %slice_bitcast_fusion.6), channel_id=1, source_target_pairs={{1,0},{2,1},{3,2},{5,4},{6,5},{7,6},{9,8},{10,9},{11,10},{13,12},{... | collective-permute-start | bytes 200 | tf_op jit(solution)/shard_map/ppermute | solution.py:32
  13.7 62.7 %copy-start.56 = (pred[2]{0:T(512)(128)(4,1)}, pred[2]{0:T(512)(128)(4,1)S(1)}, u32[]{:S(2)}) copy-start(pred[2]{0:T(512)(128)(4,1)S(1)} %get-tuple-element.660) | copy-start | bytes 10
  13.7 64.1 %copy-start.57 = (pred[2]{0:T(512)(128)(4,1)}, pred[2]{0:T(512)(128)(4,1)S(1)}, u32[]{:S(2)}) copy-start(pred[2]{0:T(512)(128)(4,1)S(1)} %get-tuple-element.658) | copy-start | bytes 10
  13.7 64.1 %copy-start.58 = (pred[2]{0:T(512)(128)(4,1)}, pred[2]{0:T(512)(128)(4,1)S(1)}, u32[]{:S(2)}) copy-start(pred[2]{0:T(512)(128)(4,1)S(1)} %get-tuple-element.662) | copy-start | bytes 10
  13.7 64.1 %copy-start.60 = (pred[2]{0:T(512)(128)(4,1)}, pred[2]{0:T(512)(128)(4,1)S(1)}, u32[]{:S(2)}) copy-start(pred[2]{0:T(512)(128)(4,1)S(1)} %get-tuple-element.659) | copy-start | bytes 10
  81.5 314.3 %copy-start.39 = (s32[128,16,16]{0,2,1:T(8,128)S(1)}, s32[128,16,16]{0,2,1:T(8,128)}, u32[]{:S(2)}) copy-start(s32[128,16,16]{0,2,1:T(8,128)} %param.37) | copy-start | bytes 393220
  81.5 315.6 %copy-start.44 = (s32[16,16]{1,0:T(8,128)S(1)}, s32[16,16]{1,0:T(8,128)}, u32[]{:S(2)}) copy-start(s32[16,16]{1,0:T(8,128)} %param.32) | copy-start | bytes 3076
  392.1 52.7 %collective-permute-start.1 = (f32[4,16]{1,0:T(4,128)S(1)}, f32[4,16]{1,0:T(4,128)S(1)}, u32[]{:S(2)}, u32[]{:S(2)}) collective-permute-start(f32[4,16]{1,0:T(4,128)S(1)} %slice_reduce_fusion), channel_id=1, source_target_pairs={{4,0},{8,4},{12,8},{16,12},{20,16},{24,20},{28,24},{5,1},{9,5},{13... | collective-permute-start | bytes 776 | tf_op jit(solution)/shard_map/ppermute | solution.py:32
  393.4 51.5 %collective-permute-start.3 = (f32[4,16]{1,0:T(4,128)S(1)}, f32[4,16]{1,0:T(4,128)S(1)}, u32[]{:S(2)}, u32[]{:S(2)}) collective-permute-start(f32[4,16]{1,0:T(4,128)S(1)} %bitcast.791), channel_id=1, source_target_pairs={{1,0},{2,1},{3,2},{5,4},{6,5},{7,6},{9,8},{10,9},{11,10},{13,12},{... | collective-permute-start | bytes 776 | tf_op jit(solution)/shard_map/ppermute | solution.py:32
  394.8 62.6 %copy-start.49 = (f32[256]{0:T(256)}, f32[256]{0:T(256)S(1)}, u32[]{:S(2)}) copy-start(f32[256]{0:T(256)S(1)} %convert_element_type.316) | copy-start | bytes 3076
  445.8 6.8 collective-permute-start.4
  448.5 5.5 collective-permute-start.5
  470.9 34.4 %copy-start.9 = (f32[8,64,32]{2,1,0:T(8,128)}, f32[8,64,32]{2,1,0:T(8,128)S(1)}, u32[]{:S(2)}) copy-start(f32[8,64,32]{2,1,0:T(8,128)S(1)} %get-tuple-element.1449) | copy-start | bytes 196612 | tf_op jit(solution)/shard_map/while
  554.0 34.4 %copy-start.9 = (f32[8,64,32]{2,1,0:T(8,128)}, f32[8,64,32]{2,1,0:T(8,128)S(1)}, u32[]{:S(2)}) copy-start(f32[8,64,32]{2,1,0:T(8,128)S(1)} %get-tuple-element.1449) | copy-start | bytes 196612 | tf_op jit(solution)/shard_map/while
  721.5 34.4 %copy-start.9 = (f32[8,64,32]{2,1,0:T(8,128)}, f32[8,64,32]{2,1,0:T(8,128)S(1)}, u32[]{:S(2)}) copy-start(f32[8,64,32]{2,1,0:T(8,128)S(1)} %get-tuple-element.1449) | copy-start | bytes 196612 | tf_op jit(solution)/shard_map/while
  805.2 34.4 %copy-start.9 = (f32[8,64,32]{2,1,0:T(8,128)}, f32[8,64,32]{2,1,0:T(8,128)S(1)}, u32[]{:S(2)}) copy-start(f32[8,64,32]{2,1,0:T(8,128)S(1)} %get-tuple-element.1449) | copy-start | bytes 196612 | tf_op jit(solution)/shard_map/while
  972.7 34.4 %copy-start.9 = (f32[8,64,32]{2,1,0:T(8,128)}, f32[8,64,32]{2,1,0:T(8,128)S(1)}, u32[]{:S(2)}) copy-start(f32[8,64,32]{2,1,0:T(8,128)S(1)} %get-tuple-element.1449) | copy-start | bytes 196612 | tf_op jit(solution)/shard_map/while
  1056.5 34.4 %copy-start.9 = (f32[8,64,32]{2,1,0:T(8,128)}, f32[8,64,32]{2,1,0:T(8,128)S(1)}, u32[]{:S(2)}) copy-start(f32[8,64,32]{2,1,0:T(8,128)S(1)} %get-tuple-element.1449) | copy-start | bytes 196612 | tf_op jit(solution)/shard_map/while
  1140.3 140.3 %copy-start.28 = (f32[1,2,128,283]{2,1,3,0:T(2,128)S(1)}, f32[1,2,128,283]{2,1,3,0:T(2,128)}, u32[]{:S(2)}) copy-start(f32[1,2,128,283]{2,1,3,0:T(2,128)} %param.41) | copy-start | bytes 869380
  1140.3 140.3 %copy-start.35 = (f32[1,2,128,283]{2,1,3,0:T(2,128)S(1)}, f32[1,2,128,283]{2,1,3,0:T(2,128)}, u32[]{:S(2)}) copy-start(f32[1,2,128,283]{2,1,3,0:T(2,128)} %param.51) | copy-start | bytes 869380
  1140.3 140.3 %copy-start.36 = (f32[1,2,128,283]{2,1,3,0:T(2,128)S(1)}, f32[1,2,128,283]{2,1,3,0:T(2,128)}, u32[]{:S(2)}) copy-start(f32[1,2,128,283]{2,1,3,0:T(2,128)} %param.46) | copy-start | bytes 869380
  1140.3 140.2 %copy-start.59 = (pred[2]{0:T(512)(128)(4,1)S(1)}, pred[2]{0:T(512)(128)(4,1)}, u32[]{:S(2)}) copy-start(pred[2]{0:T(512)(128)(4,1)} %copy-done.58) | copy-start | bytes 10
  (363 other events, 1063.1 us)
Sparse Core Ops, SparseCore 0:
  1145.7 131.2 all-reduce.10
where the time goes:
time: 1310 us; the launch traced here: 1290 us
  matrix products  350 us (27%)
  local copies, waits for them, and re-layouts  345 us (26%)
  other arithmetic  298 us (23%)
  blocking collectives  139 us (11%)
  waiting for transfers between devices  88.1 us (7%)
  loops' own time  43.7 us (3%)
  between operations  18.7 us (1%)
    another operation x100, other arithmetic  112 us
    psum x2, blocking collectives, per_device(): lax.psum((owned_parts[0], owned_parts[1], owned_parts[2], owned_parts[3],...  97.5 us
    psum x1, waiting for transfers between devices, per_device(): lax.psum((totals[0], totals[1], totals[2], totals[3], totals[4], loss_par...  87 us
    dot_general x48, matrix products, transposed(): lax.dot_general(weight, gradient, (((0,), (0,)), ((), ())), preferred_ele...  85.6 us
    dot_general x32, matrix products, field_forward(): jnp.dot(colour, view_hidden, preferred_element_type=jnp.float32)  67.2 us
    concatenate x32, local copies, waits for them, and re-layouts, encode(): jnp.concatenate([points, wavesets.reshape((6 * levels,) + points.shape[1:...  60.3 us
    dot_general x32, matrix products, field_forward(): jnp.dot(middle, hidden_one, preferred_element_type=jnp.float32)  52.3 us
    psum x1, blocking collectives, per_device(): lax.psum((totals[0], totals[1], totals[2], totals[3], totals[4], loss_par...  41.1 us
  transfers between devices with their start and end apart: 7, of which 2 were waited for; matrix products, arithmetic and copies ran while one was open for 25% of the time, Pallas kernels for 0%

commit v1 on v0

v1 whole, which is shorter than its diff:
```python
import functools
import math

import jax
import jax.numpy as jnp
from jax import lax
from jax.experimental import pallas as pl
from jax.experimental.pallas import tpu as pltpu
from jax.sharding import PartitionSpec as P

LPOS = 10
LDIR = 4
SC = 64
NT = 1024
NHIST = 64

near_plane = 2.0
far_plane = 6.0
shrink = 0.125
smooth_weight = 0.1
entropy_weight = 0.1
beta_first = 0.9
beta_second = 0.999
adam_epsilon = 1e-08
decay_rate = 0.01
learn_rate = 0.05
step_count = 10

MESH = pl.DeviceIdType.MESH
F32 = jnp.float32
BF16 = jnp.bfloat16
HIGH = lax.Precision.HIGHEST
GROUP = 8
ROWS = 512
LIMIT = 66_000_000

ROW_M, ROW_V, ROW_S, ROW_E, ROW_D = 0, 256, 384, 400, 464

PI_A = 3.140625
PI_B = 0.0009670257568359375
PI_C = math.pi - PI_A - PI_B
SIN = (-0.16666656732559204, 0.008333015255630016, -0.00019806479394901544, 2.5997517241194146e-06)
COS = (-0.5, 0.04166664183139801, -0.0013888400280848145, 2.4761729946476407e-05, -2.607421833999979e-07)


def dot(a, b, precision=None):
    return lax.dot_general(a, b, (((1,), (0,)), ((), ())), preferred_element_type=F32, precision=precision)


def dot_nt(a, b, precision=None):
    return lax.dot_general(a, b, (((1,), (1,)), ((), ())), preferred_element_type=F32, precision=precision)


def dot_tn(a, b, precision=None):
    return lax.dot_general(a, b, (((0,), (0,)), ((), ())), preferred_element_type=F32, precision=precision)


def iota(shape, axis):
    return lax.broadcasted_iota(jnp.int32, shape, axis)


def sin_cos_twice(y):
    k = jnp.round(y * (1.0 / math.pi))
    y = ((y - k * PI_A) - k * PI_B) - k * PI_C
    t = y * y
    s = y * (1.0 + t * (SIN[0] + t * (SIN[1] + t * (SIN[2] + t * SIN[3]))))
    c = 1.0 + t * (COS[0] + t * (COS[1] + t * (COS[2] + t * (COS[3] + t * COS[4]))))
    d = s + s
    return d * c, 1.0 - d * s


def code_column(row, levels, pad):
    half = row % pad
    third = 3 * levels
    wave = 3 + 6 * (half // 3) + half % 3 + jnp.where(row >= pad, 3, 0)
    if levels == LPOS:
        rest = jnp.where(row == 30, 0, jnp.where(row == 31, 1, jnp.where(row == 62, 2, -1)))
    else:
        rest = jnp.where((row >= 12) & (row < 15), row - 12, jnp.where(row == 28, -1, -2))
    return jnp.where(half < third, wave, rest)


def selector(rows, columns, levels, pad, dtype):
    return (iota((rows, columns), 1) == code_column(iota((rows, columns), 0), levels, pad)).astype(dtype)


def mesh_bits(sizes):
    bits = [("tx", 0)] if sizes["tx"] > 1 else []
    bits += [("ty", b) for b in range(sizes["ty"].bit_length() - 1)]
    bits += [("tx", b) for b in range(1, sizes["tx"].bit_length() - 1)]
    return bits


def partner_of(axis, bit):
    me = lax.axis_index(axis)
    side = (me // (1 << bit)) % 2
    return side, {axis: me + (1 - 2 * side) * (1 << bit)}


def greet(partners):
    barrier = pltpu.get_barrier_semaphore()
    for where in partners:
        pl.semaphore_signal(barrier, inc=1, device_id=where, device_id_type=MESH)
    pl.semaphore_wait(barrier, len(partners))


def all_sum(bits, least, big, arrived, whole, small, small_arrived, sems):
    send, recv, send_small, recv_small = sems
    rows = big.shape[0]
    offset, size, at = 0, rows, 0
    plan = []
    for i, (axis, bit) in enumerate(bits):
        side, where = partner_of(axis, bit)
        tiny = pltpu.make_async_remote_copy(
            small.at[i % 2], small_arrived.at[i], send_small.at[i], recv_small.at[i], device_id=where, device_id_type=MESH
        )
        tiny.start()
        halve = size // 2 >= least
        length = size // 2 if halve else size
        keep = pl.multiple_of(offset + side * length, least) if halve else offset
        give = pl.multiple_of(offset + (1 - side) * length, least) if halve else offset
        copy = pltpu.make_async_remote_copy(
            big.at[pl.ds(give, length)],
            arrived.at[pl.ds(at, length)],
            send.at[i],
            recv.at[i],
            device_id=where,
            device_id_type=MESH,
        )
        copy.start()
        tiny.wait()
        small[(i + 1) % 2] = small[i % 2] + small_arrived[i]
        copy.wait()
        big[pl.ds(keep, length)] = big[pl.ds(keep, length)] + arrived[at : at + length]
        at += length
        if halve:
            plan.append((axis, bit, offset, keep, length))
            offset, size = keep, length
    whole[pl.ds(offset, size)] = big[pl.ds(offset, size)]
    for j, (axis, bit, before, keep, length) in enumerate(reversed(plan)):
        _, where = partner_of(axis, bit)
        copy = pltpu.make_async_remote_copy(
            whole.at[pl.ds(keep, length)],
            whole.at[pl.ds(keep, length)],
            send.at[len(bits) + j],
            recv.at[len(bits) + j],
            device_id=where,
            device_id_type=MESH,
        )
        copy.start()
        copy.wait()


def sum_scratch(bits, rows, dtype):
    n = len(bits)
    return [
        pltpu.VMEM((rows, 256), dtype),
        pltpu.VMEM((2 * rows, 256), dtype),
        pltpu.VMEM((rows, 256), dtype),
        pltpu.VMEM((2, 8, 128), F32),
        pltpu.VMEM((n, 8, 128), F32),
        pltpu.SemaphoreType.DMA((2 * n,)),
        pltpu.SemaphoreType.DMA((2 * n,)),
        pltpu.SemaphoreType.DMA((n,)),
        pltpu.SemaphoreType.DMA((n,)),
    ]


def spread_kernel(bits, tiles_y, owners, rays, encoder, middle, viewer, colour, scalars, out, counts, big, arrived, whole, small, small_arrived, *sems):
    device = lax.axis_index("tx") * tiles_y + lax.axis_index("ty")
    lanes = rays.shape[1]
    choose_e = selector(64, encoder.shape[2], LPOS, 32, BF16)
    choose_d = selector(32, viewer.shape[2] - 256, LDIR, 16, BF16)

    def rounded(group, net, value):
        return jnp.where(owners[group, net] == device, value, 0.0).astype(BF16)

    for net in range(2):
        base = net * ROWS
        big[base + ROW_M : base + ROW_M + 256] = rounded(1, net, middle[net])
        views = rounded(2, net, viewer[net])
        big[base + ROW_V : base + ROW_V + 128] = views[:, :256]
        row = rounded(4, net, scalars[net : net + 1]).astype(F32)
        empty = jnp.zeros((1, 256), F32)
        block = iota((16, 256), 0)
        picked = jnp.where(block == 0, row[:, 512:768], jnp.where(block == 1, row[:, 256:512], empty))
        tail = jnp.concatenate([row[:, 768:], jnp.zeros((1, 124), F32)], 1)
        picked = jnp.where(block == 2, tail, picked)
        big[base + ROW_S : base + ROW_S + 16] = picked.astype(BF16)
        first = dot_nt(choose_e, rounded(0, net, encoder[net]))
        first = jnp.where(iota((64, 256), 0) == 63, row[:, :256], first)
        big[base + ROW_E : base + ROW_E + 64] = first.astype(BF16)
        views_d = dot_nt(choose_d, views[:, 256:])
        paint = jnp.concatenate([rounded(3, net, colour[net]).astype(F32), jnp.zeros((29, 128), F32)], 0)
        big[base + ROW_D : base + ROW_D + 32, 0:128] = views_d.astype(BF16)
        big[base + ROW_D : base + ROW_D + 32, 128:256] = paint.astype(BF16)
        big[base + ROW_D + 32 : base + ROWS] = jnp.zeros((ROWS - ROW_D - 32, 256), BF16)
    camera, mask = rays[7:8], rays[6:7]
    picks = (camera == iota((128, lanes), 0).astype(F32)) | (iota((128, lanes), 0) == 127)
    small[0] = dot_nt(jnp.broadcast_to(mask, (8, lanes)).astype(BF16), picks.astype(BF16))
    greet([partner_of(axis, bit)[1] for axis, bit in bits])
    all_sum(bits, 16, big, arrived, whole, small, small_arrived, sems)
    out[...] = whole[...]
    counts[...] = small[len(bits) % 2]


def total_kernel(bits, grads, stats, out, sums, big, arrived, whole, small, small_arrived, *sems):
    big[...] = grads[...]
    small[0] = stats[...]
    greet([partner_of(axis, bit)[1] for axis, bit in bits])
    all_sum(bits, 8, big, arrived, whole, small, small_arrived, sems)
    out[...] = whole[...]
    sums[...] = small[len(bits) % 2]


def running(block):
    row = iota(block.shape, 0)
    for shift in (1, 2, 4):
        block = block + jnp.where(row >= shift, pltpu.roll(block, shift, 0), 0.0)
    return block


def running_back(block):
    row = iota(block.shape, 0)
    for shift in (1, 2, 4):
        block = block + jnp.where(row < 8 - shift, pltpu.roll(block, 8 - shift, 0), 0.0)
    return block


def total(block):
    return jnp.sum(block, 0, keepdims=True)


def rays_kernel(
    sizes, tile, cameras, levels, bins, rays, spread, anchors, params, counts, grads, stats,
    enc, h1, h2, hv, raw, tints, depth, weight, passed, back, hist, w_e, w_m, w_mt, w_v, w_vt, w_c, w_ct, bias, per_ray,
    g_e, g_m, g_v, g_c, g_r, mine, halo, send, recv,
):
    lanes = rays.shape[1]
    points = GROUP * lanes
    tile_rows, tile_cols = tile
    tx, ty = lax.axis_index("tx"), lax.axis_index("ty")
    sides = (
        ({"tx": tx - 1}, tx > 0),
        ({"tx": tx + 1}, tx < sizes["tx"] - 1),
        ({"ty": ty - 1}, ty > 0),
        ({"ty": ty + 1}, ty < sizes["ty"] - 1),
    )
    barrier = pltpu.get_barrier_semaphore()
    expected = 0
    for where, there in sides:
        expected = expected + there.astype(jnp.int32)

        @pl.when(there)
        def _(where=where):
            pl.semaphore_signal(barrier, inc=1, device_id=where, device_id_type=MESH)

    pl.semaphore_wait(barrier, expected)

    camera, mask = rays[7:8], rays[6:7]
    picks = (camera == iota((128, lanes), 0).astype(F32)).astype(F32)
    origin = dot(anchors[...], picks, HIGH)
    heading = spread[...]
    o_main, d_main = origin[:32], heading[:32]
    row8 = iota((8, lanes), 0)
    o_last, d_last = jnp.where(row8 == 7, 1.0 / shrink, origin[32:]), heading[32:]
    row32 = iota((32, lanes), 0)
    half_pi = jnp.float32(math.pi) * 0.5
    scale = jnp.zeros((32, lanes), F32)
    for level in range(LPOS):
        scale = jnp.where((row32 >= 3 * level) & (row32 < 3 * level + 3), half_pi * (2.0**level), scale)

    row16 = iota((16, lanes), 0)
    scale_d = jnp.zeros((16, lanes), F32)
    for level in range(LDIR):
        scale_d = jnp.where((row16 >= 3 * level) & (row16 < 3 * level + 3), half_pi * (2.0**level), scale_d)
    sin_d, cos_d = sin_cos_twice(d_main[:16] * scale_d)
    top = jnp.where(row16 >= 12, jnp.where(row16 < 15, d_main[:16], 0.0), sin_d)
    bottom = jnp.where(row16 >= 12, jnp.where(row16 == 12, 1.0, 0.0), cos_d)
    view_code = jnp.concatenate([top, bottom], 0).astype(BF16)

    count = counts[...]
    mask_floor = jnp.maximum(count[0:1, 127:128], 1.0)
    inverse = 1.0 / jnp.maximum(count, 1.0)
    ray_weight = dot(inverse, picks, HIGH)[0:1] * mask / cameras
    target = rays[3:6]
    ones = jnp.full((16, points), 1.0, BF16)
    stats[...] = jnp.zeros_like(stats)
    loss = jnp.zeros((1, lanes), F32)

    for net, samples in ((0, SC), (1, levels.shape[0])):
        blocks = samples // GROUP
        base = net * ROWS
        middle = params[base + ROW_M : base + ROW_M + 256]
        w_m[...] = middle
        w_mt[...] = middle.astype(F32).T.astype(BF16)
        misc = params[base + ROW_S : base + ROW_S + 16]
        row = iota((16, 256), 0)
        misc32 = misc.astype(F32)
        sigma = jnp.where(row == 0, misc32, 0.0)
        w_v[0:128] = params[base + ROW_V : base + ROW_V + 128]
        w_v[128:144] = sigma.astype(BF16)
        views_t = params[base + ROW_V : base + ROW_V + 128].astype(F32).T
        w_vt[:, 0:128] = views_t.astype(BF16)
        sigma_t = jnp.concatenate([jnp.zeros((3, 256), F32), misc32[0:1], jnp.zeros((124, 256), F32)], 0).T
        w_vt[:, 128:144] = sigma_t[:, :16].astype(BF16)
        w_e[...] = params[base + ROW_E : base + ROW_E + 64].astype(F32).T.astype(BF16)
        last = params[base + ROW_D : base + ROW_D + 32].astype(F32)
        paint = last[:16, 128:]
        tail = misc32[2:3]
        sigma_bias = tail[:, 0:1]
        lane = iota((16, 128), 1)
        row_c = iota((16, 128), 0)
        tint_bias = jnp.zeros((16, 128), F32)
        for k in range(3):
            tint_bias = jnp.where((row_c == k) & (lane == 0), tail[:, 129 + k : 130 + k], tint_bias)
        w_c[:, 0:128] = paint.astype(BF16)
        w_c[:, 128:144] = tint_bias[:, :16].astype(BF16)
        w_ct[...] = jnp.concatenate([paint, jnp.zeros((112, 128), F32)], 0).T[:, :16].astype(BF16)
        bias[...] = jnp.broadcast_to(misc32[1:2], (128, 256)).T
        views_d = last[:, :128]
        shifted = pltpu.roll(jnp.broadcast_to(tail, (8, 256)), 255, 1)[0:1, :128]
        views_d = jnp.where(iota((32, 128), 0) == 28, shifted, views_d)
        per_ray[...] = dot_tn(views_d.astype(BF16), view_code)

        if net == 0:
            for b in range(blocks):
                at = (row8 + b * GROUP).astype(F32)
                depth[b] = near_plane + (far_plane - near_plane) * (at + 0.5) / SC
        else:
            for b in range(blocks):
                at = levels[b * GROUP : b * GROUP + GROUP].astype(F32)
                depth[b] = near_plane + (far_plane - near_plane) * (at + 0.5) / NT

        def encode(c):
            for s in range(GROUP):
                t = depth[c, s : s + 1]
                place = (o_main + t * d_main) * shrink
                wave, cowave = sin_cos_twice(place * scale)
                wave = jnp.where(row32 >= 30, place, wave)
                extra = (o_last + t * d_last) * shrink
                end = jnp.where(row8 >= 6, extra, cowave[24:])
                cowave = jnp.concatenate([cowave[:24], end], 0)
                enc[c, 0:32, s * lanes : s * lanes + lanes] = wave.astype(BF16)
                enc[c, 32:64, s * lanes : s * lanes + lanes] = cowave.astype(BF16)

        def forward(c, carry):
            one = jnp.maximum(dot(w_e[...], enc[c]).astype(BF16), 0)
            h1[c] = one
            two = dot(w_m[...], one) + jnp.tile(bias[...], (1, points // 128))
            two = jnp.maximum(two.astype(BF16), 0)
            h2[c] = two
            out = dot(w_v[...], two)
            view = out[:128] + jnp.tile(per_ray[...], (1, GROUP))
            view = jnp.maximum(view.astype(BF16), 0)
            hv[c] = view
            paint = dot(w_c[...], jnp.concatenate([view, ones], 0))
            for s in range(GROUP):
                part = slice(s * lanes, s * lanes + lanes)
                for k in range(3):
                    raw[k, c, s : s + 1] = paint[k : k + 1, part]
                raw[3, c, s : s + 1] = out[128:129, part]
            encode(jnp.minimum(c + 1, blocks - 1))
            return carry

        encode(0)
        lax.fori_loop(0, blocks, forward, 0)

        before = jnp.zeros((1, lanes), F32)
        colour = [jnp.zeros((8, lanes), F32) for _ in range(3)]
        far, opaque = jnp.zeros((8, lanes), F32), jnp.zeros((8, lanes), F32)

        def spacing(b):
            t = depth[b]
            after = depth[b + 1, 0:1] if b + 1 < blocks else jnp.full((1, lanes), far_plane, F32)
            return jnp.where(row8 == 7, after, pltpu.roll(t, 7, 0)) - t

        for b in range(blocks):
            zs = raw[3, b] + sigma_bias
            density = jnp.maximum(zs, 0.0) + jnp.log1p(jnp.exp(-jnp.abs(zs)))
            q = density * spacing(b)
            inclusive = running(q) + before
            before = inclusive[7:8]
            lit = jnp.exp(-(inclusive - q))
            w = lit * (1.0 - jnp.exp(-q))
            weight[b] = w
            passed[b] = jnp.exp(-inclusive)
            if net == 1:
                back[3, b] = density * mask
            for k in range(3):
                tint = jax.nn.sigmoid(raw[k, b])
                tints[k, b] = tint
                colour[k] = colour[k] + w * tint
            far = far + w * depth[b]
            opaque = opaque + w
        colour = [total(x) for x in colour]
        far, opaque = total(far), total(opaque)
        miss = [colour[k] - target[k : k + 1] for k in range(3)]
        loss = loss + ray_weight * (miss[0] * miss[0] + miss[1] * miss[1] + miss[2] * miss[2])
        seed = [2.0 * ray_weight * miss[k] for k in range(3)]
        seed_depth = seed_opaque = None
        if net == 1:
            for k in range(3):
                mine[k : k + 1] = colour[k]
            mine[3:4] = far
            mine[4:5] = mask
            mine[5:8] = jnp.zeros((3, lanes), F32)
            for i, (where, there) in enumerate(sides):

                @pl.when(there)
                def _(i=i, where=where):
                    pltpu.make_async_remote_copy(
                        mine, halo.at[i], send.at[i], recv.at[i], device_id=where, device_id_type=MESH
                    ).start()

            def count_bin(b, carry):
                sums = jnp.zeros((8, lanes), F32)
                for s in range(blocks):
                    sums = sums + jnp.where(bins[s * GROUP : s * GROUP + GROUP] == b, back[3, s], 0.0)
                hist[b] = sums
                return carry

            lax.fori_loop(0, NHIST, count_bin, 0)
            sums = jnp.sum(hist[...], 1)
            stats[0:1, 0:NHIST] = dot_nt(jnp.full((8, lanes), 1.0, F32), sums, HIGH)[0:1]
            solid = 0.01 + 0.98 * opaque
            entropy = -mask * (solid * jnp.log(solid) + (1.0 - solid) * jnp.log(1.0 - solid))
            seed_opaque = -(entropy_weight / mask_floor) * mask * 0.98 * (jnp.log(solid) - jnp.log(1.0 - solid))
            for i, (where, there) in enumerate(sides):
                j = i ^ 1

                @pl.when(there)
                def _(i=i, j=j, where=where):
                    pltpu.make_async_remote_copy(
                        mine, halo.at[i], send.at[i], recv.at[i], device_id=where, device_id_type=MESH
                    ).wait_send()
                    pltpu.make_async_remote_copy(
                        mine, halo.at[j], send.at[i], recv.at[j], device_id=where, device_id_type=MESH
                    ).wait_recv()

            values = mine[...]
            lane = iota((8, lanes), 1)
            col, tile_row = lane % tile_cols, lane // tile_cols

            def beside(i, inner, shift, wrap):
                other = jnp.where(
                    inner, pltpu.roll(values, shift % lanes, 1), pltpu.roll(halo[i ^ 1], wrap % lanes, 1)
                )
                known = inner | sides[i][1]
                return jnp.where(known, other, 0.0)

            smooth = jnp.zeros((8, lanes), F32)
            pull = jnp.zeros((8, lanes), F32)
            for i, inner, shift, wrap in (
                (0, col > 0, 1, 1 - tile_cols),
                (1, col < tile_cols - 1, -1, tile_cols - 1),
                (2, tile_row > 0, tile_cols, tile_cols - lanes),
                (3, tile_row < tile_rows - 1, -tile_cols, lanes - tile_cols),
            ):
                other = beside(i, inner, shift, wrap)
                pair = other[4:5] * mask
                gap = jnp.where(row8 < 4, values - other, 0.0)
                pull = pull + pair * gap
                if i % 2 == 1:
                    smooth = smooth + pair * gap * gap
            smooth_scale = 2.0 * smooth_weight / mask_floor
            pull = smooth_scale * pull
            seed = [seed[k] + pull[k : k + 1] for k in range(3)]
            seed_depth = pull[3:4]
            loss = loss + (smooth_weight * total(smooth) + entropy_weight * entropy) / mask_floor

        later = jnp.zeros((1, lanes), F32)
        for b in reversed(range(blocks)):
            w = weight[b]
            tint = [tints[k, b] for k in range(3)]
            pulled = seed[0] * tint[0] + seed[1] * tint[1] + seed[2] * tint[2]
            if net == 1:
                pulled = pulled + seed_depth * depth[b] + seed_opaque
            weighted = pulled * w
            onward = running_back(weighted) + later
            later = onward[0:1]
            dq = pulled * passed[b] - (onward - weighted)
            zs = raw[3, b] + sigma_bias
            back[3, b] = dq * spacing(b) * jax.nn.sigmoid(zs)
            for k in range(3):
                back[k, b] = w * seed[k] * tint[k] * (1.0 - tint[k])

        g_e[...] = jnp.zeros_like(g_e)
        g_m[...] = jnp.zeros_like(g_m)
        g_v[...] = jnp.zeros_like(g_v)
        g_c[...] = jnp.zeros_like(g_c)
        g_r[...] = jnp.zeros_like(g_r)

        def backward(c, carry):
            parts = []
            for s in range(GROUP):
                parts.append(jnp.concatenate([back[k, c, s : s + 1] for k in range(4)] + [jnp.zeros((12, lanes), F32)], 0))
            gate = jnp.concatenate(parts, 1).astype(BF16)
            view = hv[c]
            gv = jnp.where(view > 0, dot(w_ct[...], gate).astype(BF16), 0)
            sums = g_r[...]
            for s in range(GROUP):
                sums = sums + gv[:, s * lanes : s * lanes + lanes].astype(F32)
            g_r[...] = sums
            g_c[...] += dot_nt(gate, jnp.concatenate([view, ones], 0))
            both = jnp.concatenate([gv, gate], 0)
            two = h2[c]
            g_v[...] += dot_nt(both, two)
            g2 = jnp.where(two > 0, dot(w_vt[...], both).astype(BF16), 0)
            one = h1[c]
            g_m[...] += dot_nt(jnp.concatenate([one, ones], 0), g2)
            g1 = jnp.where(one > 0, dot(w_mt[...], g2).astype(BF16), 0)
            g_e[...] += dot_nt(enc[c], g1)
            return carry

        lax.fori_loop(0, blocks, backward, 0)

        grads[base + ROW_M : base + ROW_M + 256] = g_m[0:256]
        grads[base + ROW_V : base + ROW_V + 128] = g_v[0:128]
        row = iota((16, 256), 0)
        lane = iota((16, 256), 1)
        grad_misc = jnp.where(row == 0, g_v[131:132], jnp.where(row == 1, g_m[256:257], 0.0))
        sums_c = g_c[:, 128:129]
        for k, spot in ((3, 0), (0, 129), (1, 130), (2, 131)):
            grad_misc = jnp.where((row == 2) & (lane == spot), sums_c[k : k + 1], grad_misc)
        grads[base + ROW_S : base + ROW_S + 16] = grad_misc
        grads[base + ROW_E : base + ROW_E + 64] = g_e[...]
        grads[base + ROW_D : base + ROW_D + 32, 0:128] = dot_nt(view_code.astype(F32), g_r[...], HIGH)
        grads[base + ROW_D : base + ROW_D + 32, 128:256] = jnp.concatenate([g_c[:, :128], jnp.zeros((16, 128), F32)], 0)
        grads[base + ROW_D + 32 : base + ROWS] = jnp.zeros((ROWS - ROW_D - 32, 256), F32)
    fold = loss[:, :128]
    for k in range(1, lanes // 128):
        fold = fold + loss[:, k * 128 : k * 128 + 128]
    stats[1:2] = fold


def adamw_update(weight, moment, square, gradient):
    moment_next = beta_first * moment + (1.0 - beta_first) * gradient
    square_next = beta_second * square + (1.0 - beta_second) * gradient * gradient
    first_hat = moment_next / (1.0 - beta_first**step_count)
    second_hat = square_next / (1.0 - beta_second**step_count)
    weight_next = weight - learn_rate * (
        first_hat / (jnp.sqrt(second_hat) + adam_epsilon) + decay_rate * weight
    )
    return (weight_next, moment_next, square_next)


def update_kernel(tiles_y, owners, grads, stats, counts, *refs):
    masters, moments, squares = refs[0:5], refs[5:10], refs[10:15]
    loss, histogram = refs[15], refs[16]
    nexts, next_moments, next_squares = refs[17:22], refs[22:27], refs[27:32]
    device = lax.axis_index("tx") * tiles_y + lax.axis_index("ty")
    mask_floor = jnp.maximum(counts[0:1, 127:128], 1.0)
    histogram[...] = stats[0:1] / mask_floor
    loss[...] = jnp.sum(stats[1:2], 1, keepdims=True)
    choose_e = selector(64, masters[0].shape[2], LPOS, 32, F32)
    choose_d = selector(32, masters[2].shape[2] - 256, LDIR, 16, F32)

    def step(group, net, at, gradient):
        owned = owners[group, net] == device
        old = [ref[at] for ref in (masters[group], moments[group], squares[group])]
        new = adamw_update(*old, gradient)
        for ref, was, now in zip((nexts[group], next_moments[group], next_squares[group]), old, new):
            ref[at] = jnp.where(owned, now, was)

    for net in range(2):
        base = net * ROWS
        step(0, net, (net,), dot_tn(grads[base + ROW_E : base + ROW_E + 64], choose_e, HIGH))
        step(1, net, (net,), grads[base + ROW_M : base + ROW_M + 256].T)
        step(2, net, (net, slice(None), slice(0, 256)), grads[base + ROW_V : base + ROW_V + 128])
        last = grads[base + ROW_D : base + ROW_D + 32]
        step(2, net, (net, slice(None), slice(256, 283)), dot_tn(last[:, :128], choose_d, HIGH))
        step(3, net, (net,), last[0:3, 128:])
        misc = grads[base + ROW_S : base + ROW_S + 16]
        spot = slice(net, net + 1)
        step(4, net, (spot, slice(0, 256)), grads[base + ROW_E + 63 : base + ROW_E + 64])
        step(4, net, (spot, slice(256, 512)), misc[1:2])
        step(4, net, (spot, slice(512, 768)), misc[0:1])
        views = jnp.concatenate([last[28:29, :128], jnp.zeros((1, 128), F32)], 1)
        views = pltpu.roll(jnp.broadcast_to(views, (8, 256)), 1, 1)[0:1]
        step(4, net, (spot, slice(768, 900)), (misc[2:3] + views)[:, :132])


VMEM_SPEC = pl.BlockSpec(memory_space=pltpu.VMEM)
SMEM_SPEC = pl.BlockSpec(memory_space=pltpu.SMEM)


def per_device(sizes, camera, ray_mask, ray_direction, anchors, target, fine_levels, density_bins, owners, *trees):
    masters = [x[0] for x in trees[0:5]]
    moments = [x[0] for x in trees[5:10]]
    squares = [x[0] for x in trees[10:15]]
    tile = camera.shape
    lanes = tile[0] * tile[1]
    cameras = anchors.shape[1]
    samples = fine_levels.shape[0]
    bits = mesh_bits(sizes)
    levels = fine_levels.reshape(samples, lanes)
    bins = density_bins.reshape(samples, lanes)
    direction = ray_direction.reshape(3, lanes)
    rays = jnp.concatenate(
        [
            direction,
            target.reshape(3, lanes),
            ray_mask.reshape(1, lanes).astype(F32),
            camera.reshape(1, lanes).astype(F32),
        ],
        0,
    )

    def widened(rows):
        tall = jnp.concatenate([rows] * 11, 0)[:32]
        gap = jnp.zeros((6,) + rows.shape[1:], F32)
        return jnp.concatenate([tall, gap, rows[2:3], gap[:1]], 0)

    heading = widened(direction)
    centres = jnp.pad(widened(anchors), ((0, 0), (0, 128 - cameras)))

    params, counts = pl.pallas_call(
        functools.partial(spread_kernel, bits, sizes["ty"]),
        out_shape=(jax.ShapeDtypeStruct((2 * ROWS, 256), BF16), jax.ShapeDtypeStruct((8, 128), F32)),
        in_specs=[SMEM_SPEC] + [VMEM_SPEC] * 6,
        out_specs=(VMEM_SPEC, VMEM_SPEC),
        scratch_shapes=sum_scratch(bits, 2 * ROWS, BF16),
        compiler_params=pltpu.CompilerParams(collective_id=0, has_side_effects=True),
        name="spread",
    )(owners, rays, *masters)

    points = GROUP * lanes
    blocks = samples // GROUP
    grads, stats = pl.pallas_call(
        functools.partial(rays_kernel, sizes, tile, cameras),
        out_shape=(jax.ShapeDtypeStruct((2 * ROWS, 256), F32), jax.ShapeDtypeStruct((8, 128), F32)),
        in_specs=[VMEM_SPEC] * 7,
        out_specs=(VMEM_SPEC, VMEM_SPEC),
        scratch_shapes=[
            pltpu.VMEM((blocks, 64, points), BF16),
            pltpu.VMEM((blocks, 256, points), BF16),
            pltpu.VMEM((blocks, 256, points), BF16),
            pltpu.VMEM((blocks, 128, points), BF16),
            pltpu.VMEM((4, blocks, GROUP, lanes), F32),
            pltpu.VMEM((3, blocks, GROUP, lanes), F32),
            pltpu.VMEM((blocks, GROUP, lanes), F32),
            pltpu.VMEM((blocks, GROUP, lanes), F32),
            pltpu.VMEM((blocks, GROUP, lanes), F32),
            pltpu.VMEM((4, blocks, GROUP, lanes), F32),
            pltpu.VMEM((NHIST, 8, lanes), F32),
            pltpu.VMEM((256, 64), BF16),
            pltpu.VMEM((256, 256), BF16),
            pltpu.VMEM((256, 256), BF16),
            pltpu.VMEM((144, 256), BF16),
            pltpu.VMEM((256, 144), BF16),
            pltpu.VMEM((16, 144), BF16),
            pltpu.VMEM((128, 16), BF16),
            pltpu.VMEM((256, 128), F32),
            pltpu.VMEM((128, lanes), F32),
            pltpu.VMEM((64, 256), F32),
            pltpu.VMEM((272, 256), F32),
            pltpu.VMEM((144, 256), F32),
            pltpu.VMEM((16, 144), F32),
            pltpu.VMEM((128, lanes), F32),
            pltpu.VMEM((8, lanes), F32),
            pltpu.VMEM((4, 8, lanes), F32),
            pltpu.SemaphoreType.DMA((4,)),
            pltpu.SemaphoreType.DMA((4,)),
        ],
        compiler_params=pltpu.CompilerParams(collective_id=1, has_side_effects=True, vmem_limit_bytes=LIMIT),
        name="rays",
    )(levels, bins, rays, heading, centres, params, counts)

    grads, stats = pl.pallas_call(
        functools.partial(total_kernel, bits),
        out_shape=(jax.ShapeDtypeStruct((2 * ROWS, 256), F32), jax.ShapeDtypeStruct((8, 128), F32)),
        in_specs=[VMEM_SPEC] * 2,
        out_specs=(VMEM_SPEC, VMEM_SPEC),
        scratch_shapes=sum_scratch(bits, 2 * ROWS, F32),
        compiler_params=pltpu.CompilerParams(collective_id=2, has_side_effects=True),
        name="total",
    )(grads, stats)

    states = masters + moments + squares
    results = pl.pallas_call(
        functools.partial(update_kernel, sizes["ty"]),
        out_shape=[jax.ShapeDtypeStruct((1, 1), F32), jax.ShapeDtypeStruct((1, 128), F32)]
        + [jax.ShapeDtypeStruct(x.shape, F32) for x in states],
        in_specs=[SMEM_SPEC] + [VMEM_SPEC] * 18,
        out_specs=[VMEM_SPEC] * 17,
        name="update",
    )(owners, grads, stats, counts, *states)
    return (results[0][0, 0], results[1][0, :NHIST]) + tuple(x[None] for x in results[2:])


def solution(mesh):
    sizes = dict(mesh.shape)
    tiled, tiled3 = P("ty", "tx"), P(None, "ty", "tx")
    slots = P(("tx", "ty"), None, None, None)
    trees = (slots, slots, slots, slots, P(("tx", "ty"), None, None))
    return jax.shard_map(
        functools.partial(per_device, sizes),
        mesh=mesh,
        in_specs=(tiled, tiled, tiled3, P(), tiled3, tiled3, tiled3, P()) + trees * 3,
        out_specs=(P(), P()) + trees * 3,
        check_vma=False,
    )
```

time: 1310 us -> 201 us (0.15); the launches traced: 1290 us -> 200 us
  matrix products: 350 us -> 0 us
  local copies, waits for them, and re-layouts: 345 us -> 24.2 us
  other arithmetic: 298 us -> 1.39 us
  Pallas kernels: 0 us -> 173 us
  blocking collectives: 139 us -> 0 us
  waiting for transfers between devices: 88.1 us -> 0 us
  loops' own time: 43.7 us -> 0 us
  between operations: 18.7 us -> 0.8 us
    dot_general x305 -> x0, matrix products: 350 us -> none  [the longest x48 85.6 us: transposed(): lax.dot_general(weight, gradient, (((0,), (0,)), ((), ())), preferred_ele...]
    pallas_call x0 -> x4, Pallas kernels: none -> 173 us  [the longest x1 88.3 us: per_device(): pl.pallas_call(functools.partial(rays_kernel, sizes, tile, cameras), out_...]
    another operation x212 -> x0, other arithmetic: 140 us -> none
    psum x3 -> x0, blocking collectives: 139 us -> none  [the longest x2 97.5 us: per_device(): lax.psum((owned_parts[0], owned_parts[1], owned_parts[2], owned_parts[3],...]
    psum x1 -> x0, waiting for transfers between devices: 87 us -> none  [per_device(): lax.psum((totals[0], totals[1], totals[2], totals[3], totals[4], loss_par...]
    concatenate x67 -> x4, local copies, waits for them, and re-layouts: 83.8 us -> 0.78 us  [the longest x2 0.63 us: widened(): tall = jnp.concatenate([rows] * 11, 0)[:32]]
    convert_element_type x57 -> x2, other arithmetic: 51.1 us -> 0.01 us  [the longest x1 0.01 us: per_device(): camera.reshape(1, lanes).astype(F32)]
    slice x73 -> x6, local copies, waits for them, and re-layouts: 45.3 us -> 0.79 us  [the longest x4 0.78 us: widened(): return jnp.concatenate([tall, gap, rows[2:3], gap[:1]], 0)]
  transfers between devices with their start and end apart: 7 -> 0, of which waited for: 2 -> 0; matrix products, arithmetic and copies ran while one was open for 25% -> 0% of each run, Pallas kernels for 0% -> 0%
where the time goes in v1:
time: 201 us; the launch traced here: 200 us
  Pallas kernels  173 us (86%)
  local copies, waits for them, and re-layouts  24.2 us (12%)
    pallas_call x1, Pallas kernels, per_device(): pl.pallas_call(functools.partial(rays_kernel, sizes, tile, cameras), out_...  88.3 us
    pallas_call x1, Pallas kernels, per_device(): pl.pallas_call(functools.partial(total_kernel, bits), out_shape=(jax.Shap...  42.9 us
    pallas_call x1, Pallas kernels, per_device(): pl.pallas_call(functools.partial(spread_kernel, bits, sizes['ty']), out_s...  37 us
    unnamed x65, local copies, waits for them, and re-layouts  17.6 us
    pallas_call x1, Pallas kernels, per_device(): pl.pallas_call(functools.partial(update_kernel, sizes['ty']), out_shape=[...  5.26 us

profile of v1, /device:TPU:0, one launch (start us, length us, event | category | flops | bytes accessed | tf_op | source)
XLA Modules:
  0.0 199.8 jit_solution(5730695239578413752)
XLA Ops:
  1.4 0.7 copy.74.owners
  2.1 0.8 reshape.77
  5.7 0.7 slice-done
  8.1 0.6 pad.4.anchors
  9.1 0.7 maximum_maximum_fusion.spread
  9.8 0.8 copy.66.levels
  10.7 0.8 copy.67.bins
  11.6 0.8 copy.62
  12.5 0.8 copy.68
  13.4 0.8 copy.71
  14.3 0.9 copy.63
  15.3 0.9 copy.69
  16.2 0.9 copy.72
  17.2 37.0 %spread.1 = (bf16[1024,256]{1,0:T(8,128)(2,1)}, f32[8,128]{1,0:T(8,128)}) custom-call(s32[5,2]{1,0:T(8,128)} %copy.74.owners, f32[8,256]{1,0:T(8,128)} %pad_maximum_fusion.rays, f32[2,256,63]{2,1,0:T(8,128)} %bitcast.43, f32[2,256,256]{2,1,0:T(8,128)} %bitcast.45, f32[2,128,283]{2,1,0:T(8,128)} %bitcast.41, f32[2,3,128]{2,1,0:T(4,128)} %bitcast.61, ...), custom_call_target="tpu_custom_call" | custom-call | tf_op jit(solution)/shard_map/spread/pallas_call | solution.py:618
  54.2 88.3 %rays.1 = (f32[1024,256]{1,0:T(8,128)}, f32[8,128]{1,0:T(8,128)}) custom-call(s32[128,256]{1,0:T(8,128)} %copy.66.levels, s32[128,256]{1,0:T(8,128)} %copy.67.bins, f32[8,256]{1,0:T(8,128)} %pad_maximum_fusion.rays, f32[40,256]{1,0:T(8,128)} %maximum_maximum_fusion.spread, f32[40,128]{1,0:T(8,128)} %pad.4.anchors, ...), custom_call_target="tpu_custom_call" | custom-call | tf_op jit(solution)/shard_map/rays/pallas_call | solution.py:630
  142.5 42.9 %total.1 = (f32[1024,256]{1,0:T(8,128)}, f32[8,128]{1,0:T(8,128)}) custom-call(f32[1024,256]{1,0:T(8,128)} %get-tuple-element.42.grads, f32[8,128]{1,0:T(8,128)} %get-tuple-element.43.stats), custom_call_target="tpu_custom_call" | custom-call | tf_op jit(solution)/shard_map/total/pallas_call | solution.py:670
  185.4 5.3 %update.1 = (f32[1,1]{1,0:T(1,128)}, f32[1,128]{1,0:T(1,128)}, f32[2,256,63]{2,1,0:T(8,128)}, f32[2,256,256]{2,1,0:T(8,128)}, f32[2,128,283]{2,1,0:T(8,128)}, /*...) custom-call(s32[5,2]{1,0:T(8,128)} %copy.74.owners, ...), custom_call_target="tpu_custom_call" | custom-call | tf_op jit(solution)/shard_map/update/pallas_call | solution.py:681
  190.7 1.2 slice_bitcast_fusion
  191.9 1.8 copy.75
  195.4 0.8 copy.78
  196.2 0.8 copy.81
  197.0 0.9 copy.76
  198.0 0.9 copy.79
  199.0 0.9 copy.82
  (70 shorter events, 8.1 us)
Async XLA Ops:
  0.7 0.8 copy-start.23
  0.7 0.7 copy-start.8
  0.7 2.3 %copy-start.14 = (f32[3,16,16]{2,1,0:T(8,128)S(1)}, f32[3,16,16]{2,1,0:T(8,128)}, u32[]{:S(2)}) copy-start(f32[3,16,16]{2,1,0:T(8,128)} %param.27) | copy-start | bytes 9220
  2.9 0.7 copy-start.20
  3.6 0.7 copy-start.15
  4.3 0.7 copy-start.16
  5.7 0.7 slice-start
  6.4 0.7 copy-start.22
  8.1 1.7 copy-start.9
  9.8 0.9 copy-start.10
  10.7 0.9 copy-start.11
  11.6 0.9 copy-start.12
  12.5 0.9 copy-start.13
  13.4 1.0 copy-start.3
  14.3 1.0 copy-start.4
  15.3 1.0 copy-start.5
  190.7 4.7 %copy-start.7 = (f32[2,256,63]{2,1,0:T(8,128)S(1)}, f32[2,256,63]{2,1,0:T(8,128)}, u32[]{:S(2)}) copy-start(f32[2,256,63]{2,1,0:T(8,128)} %get-tuple-element.53) | copy-start | bytes 387076
  191.9 1.8 copy-start.19
  191.9 2.3 %copy-start.18 = (f32[2,3,128]{2,1,0:T(4,128)S(1)}, f32[2,3,128]{2,1,0:T(4,128)}, u32[]{:S(2)}) copy-start(f32[2,3,128]{2,1,0:T(4,128)} %get-tuple-element.56) | copy-start | bytes 9220
  191.9 2.9 %copy-start.17 = (f32[2,3,128]{2,1,0:T(4,128)S(1)}, f32[2,3,128]{2,1,0:T(4,128)}, u32[]{:S(2)}) copy-start(f32[2,3,128]{2,1,0:T(4,128)} %get-tuple-element.61) | copy-start | bytes 9220
  193.6 2.5 %copy-start.6 = (f32[2,256,63]{2,1,0:T(8,128)S(1)}, f32[2,256,63]{2,1,0:T(8,128)}, u32[]{:S(2)}) copy-start(f32[2,256,63]{2,1,0:T(8,128)} %get-tuple-element.58) | copy-start | bytes 387076
  194.8 2.1 %copy-start.2 = (f32[2,128,283]{2,1,0:T(8,128)S(1)}, f32[2,128,283]{2,1,0:T(8,128)}, u32[]{:S(2)}) copy-start(f32[2,128,283]{2,1,0:T(8,128)} %get-tuple-element.50) | copy-start | bytes 869380
  197.0 1.0 copy-start.1
  198.0 1.0 copy-start
  (1 other events, 0.7 us)

commit v2 on v1

v2 whole, which is shorter than its diff:
```python
import functools
import math

import jax
import jax.numpy as jnp
from jax import lax
from jax.experimental import pallas as pl
from jax.experimental.pallas import tpu as pltpu
from jax.sharding import PartitionSpec as P

LPOS = 10
LDIR = 4
SC = 64
NT = 1024
NHIST = 64

near_plane = 2.0
far_plane = 6.0
shrink = 0.125
smooth_weight = 0.1
entropy_weight = 0.1
beta_first = 0.9
beta_second = 0.999
adam_epsilon = 1e-08
decay_rate = 0.01
learn_rate = 0.05
step_count = 10

MESH = pl.DeviceIdType.MESH
F32 = jnp.float32
BF16 = jnp.bfloat16
HIGH = lax.Precision.HIGHEST
GROUP = 8
CHUNK = 8
ROWS = 512
LIMIT = 66_000_000

ROW_M, ROW_V, ROW_S, ROW_E, ROW_D = 0, 256, 384, 400, 464

PI_A = 3.140625
PI_B = 0.0009670257568359375
PI_C = math.pi - PI_A - PI_B
SIN = (-0.16666656732559204, 0.008333015255630016, -0.00019806479394901544, 2.5997517241194146e-06)
COS = (-0.5, 0.04166664183139801, -0.0013888400280848145, 2.4761729946476407e-05, -2.607421833999979e-07)


def dot(a, b, precision=None):
    return lax.dot_general(a, b, (((1,), (0,)), ((), ())), preferred_element_type=F32, precision=precision)


def dot_nt(a, b, precision=None):
    return lax.dot_general(a, b, (((1,), (1,)), ((), ())), preferred_element_type=F32, precision=precision)


def dot_tn(a, b, precision=None):
    return lax.dot_general(a, b, (((0,), (0,)), ((), ())), preferred_element_type=F32, precision=precision)


def iota(shape, axis):
    return lax.broadcasted_iota(jnp.int32, shape, axis)


def sin_cos_twice(y):
    k = jnp.round(y * (1.0 / math.pi))
    y = ((y - k * PI_A) - k * PI_B) - k * PI_C
    t = y * y
    s = y * (1.0 + t * (SIN[0] + t * (SIN[1] + t * (SIN[2] + t * SIN[3]))))
    c = 1.0 + t * (COS[0] + t * (COS[1] + t * (COS[2] + t * (COS[3] + t * COS[4]))))
    d = s + s
    return d * c, 1.0 - d * s


def code_column(row, levels, pad):
    half = row % pad
    third = 3 * levels
    wave = 3 + 6 * (half // 3) + half % 3 + jnp.where(row >= pad, 3, 0)
    if levels == LPOS:
        rest = jnp.where(row == 30, 0, jnp.where(row == 31, 1, jnp.where(row == 62, 2, -1)))
    else:
        rest = jnp.where((row >= 12) & (row < 15), row - 12, jnp.where(row == 28, -1, -2))
    return jnp.where(half < third, wave, rest)


def selector(rows, columns, levels, pad, dtype):
    return (iota((rows, columns), 1) == code_column(iota((rows, columns), 0), levels, pad)).astype(dtype)


class Members:
    def __init__(self, axis, count, spread):
        self.axis, self.count, self.spread = axis, count, spread

    def place(self):
        return (lax.axis_index(self.axis) // self.spread) % self.count

    def peer(self, step):
        me = self.place()
        other = (me + step) % self.count
        return other, {self.axis: lax.axis_index(self.axis) + (other - me) * self.spread}


def groups_of(sizes):
    cores = 2 if sizes["tx"] % 2 == 0 else 1
    groups = [Members("tx", cores, 1), Members("ty", sizes["ty"], 1), Members("tx", sizes["tx"] // cores, cores)]
    return [g for g in groups if g.count > 1]


def plan_of(groups, rows, least):
    plan = []
    for group in groups:
        after = rows // group.count if rows % (group.count * least) == 0 else rows
        plan.append((group, rows, after))
        rows = after
    return plan


def sum_scratch(plan, dtype, width=256):
    copies = sum(group.count - 1 for group, _, _ in plan)
    rows = plan[0][1]
    return (
        [pltpu.VMEM((rows, width), dtype), pltpu.VMEM((rows, width), dtype)]
        + [pltpu.VMEM((group.count, after, width), dtype) for group, _, after in plan]
        + [pltpu.VMEM((after, width), dtype) for _, _, after in plan]
        + [pltpu.SemaphoreType.DMA((2 * copies,)), pltpu.SemaphoreType.DMA((2 * copies,))]
    )


class Sum:
    def __init__(self, plan, least, refs):
        n = len(plan)
        self.plan, self.least = plan, least
        self.source, self.whole = refs[0], refs[1]
        self.landing, self.part = refs[2 : 2 + n], refs[2 + n : 2 + 2 * n]
        self.send, self.recv = refs[2 + 2 * n :]
        self.steps = 2 * n + 1

    def rows_at(self, start, length):
        return pl.ds(pl.multiple_of(start, self.least), length)

    def offsets(self):
        at, result = 0, [0]
        for group, before, after in self.plan:
            if after != before:
                at = at + group.place() * after
            result.append(at)
        return result

    def base(self, stage, back):
        copies = [group.count - 1 for group, _, _ in self.plan]
        return sum(copies[:stage]) + (sum(copies) if back else 0)

    def scatter(self, stage):
        group, before, after = self.plan[stage]
        held = self.source if stage == 0 else self.part[stage - 1]
        copies = []
        for step in range(1, group.count):
            other, where = group.peer(step)
            k = self.base(stage, False) + step - 1
            piece = held if after == before else held.at[self.rows_at(other * after, after)]
            copies.append(
                pltpu.make_async_remote_copy(
                    piece,
                    self.landing[stage].at[group.place()],
                    self.send.at[k],
                    self.recv.at[k],
                    device_id=where,
                    device_id_type=MESH,
                )
            )
        return copies

    def gather(self, stage):
        group, before, after = self.plan[stage]
        if after == before:
            return []
        mine = self.rows_at(self.offsets()[stage + 1], after)
        copies = []
        for step in range(1, group.count):
            _, where = group.peer(step)
            k = self.base(stage, True) + step - 1
            copies.append(
                pltpu.make_async_remote_copy(
                    self.whole.at[mine],
                    self.whole.at[mine],
                    self.send.at[k],
                    self.recv.at[k],
                    device_id=where,
                    device_id_type=MESH,
                )
            )
        return copies

    def step(self, k):
        n = len(self.plan)
        if 0 < k <= n:
            stage = k - 1
            group, before, after = self.plan[stage]
            held = self.source if stage == 0 else self.part[stage - 1]
            for copy in self.scatter(stage):
                copy.wait()
            own = held[...] if after == before else held[self.rows_at(group.place() * after, after)]
            self.landing[stage][group.place()] = own
            total = self.landing[stage][0]
            for j in range(1, group.count):
                total = total + self.landing[stage][j]
            self.part[stage][...] = total
            if stage == n - 1:
                self.whole[self.rows_at(self.offsets()[n], after)] = total
        elif k > n:
            for copy in self.gather(2 * n - k):
                copy.wait()
        if k < n:
            for copy in self.scatter(k):
                copy.start()
        elif k < 2 * n:
            for copy in self.gather(2 * n - 1 - k):
                copy.start()


def greet(groups, sides):
    barrier = pltpu.get_barrier_semaphore()
    expected = 0
    for group in groups:
        for step in range(1, group.count):
            pl.semaphore_signal(barrier, inc=1, device_id=group.peer(step)[1], device_id_type=MESH)
            expected = expected + 1
    for where, there in sides:
        expected = expected + there.astype(jnp.int32)

        @pl.when(there)
        def _(where=where):
            pl.semaphore_signal(barrier, inc=1, device_id=where, device_id_type=MESH)

    pl.semaphore_wait(barrier, expected)


def running(block):
    row = iota(block.shape, 0)
    for shift in (1, 2, 4):
        block = block + jnp.where(row >= shift, pltpu.roll(block, shift, 0), 0.0)
    return block


def running_back(block):
    row = iota(block.shape, 0)
    for shift in (1, 2, 4):
        block = block + jnp.where(row < 8 - shift, pltpu.roll(block, 8 - shift, 0), 0.0)
    return block


def total(block):
    return jnp.sum(block, 0, keepdims=True)


def pack(owned, net, choose_e, choose_d, big, encoder, middle, viewer, colour, scalars):
    def rounded(group, value):
        return jnp.where(owned[group], value, 0.0).astype(BF16)

    big[ROW_M : ROW_M + 256] = rounded(1, middle[net])
    views = rounded(2, viewer[:, net, :])
    big[ROW_V : ROW_V + 128, 0:128] = views[0:128]
    big[ROW_V : ROW_V + 128, 128:256] = views[128:256]
    row = rounded(4, scalars[net : net + 1]).astype(F32)
    block = iota((16, 256), 0)
    tail = jnp.concatenate([row[:, 768:], jnp.zeros((1, 124), F32)], 1)
    picked = jnp.where(block == 0, row[:, 512:768], jnp.where(block == 1, row[:, 256:512], 0.0))
    big[ROW_S : ROW_S + 16] = jnp.where(block == 2, tail, picked).astype(BF16)
    first = dot(choose_e, rounded(0, encoder[:, net, :]))
    first = jnp.where(iota((64, 256), 0) == 63, row[:, :256], first)
    big[ROW_E : ROW_E + 64] = first.astype(BF16)
    big[ROW_D : ROW_D + 32, 0:128] = dot(choose_d, views[256:]).astype(BF16)
    paint = jnp.concatenate([rounded(3, colour[:, net, :]).astype(F32), jnp.zeros((29, 128), F32)], 0)
    big[ROW_D : ROW_D + 32, 128:256] = paint.astype(BF16)
    big[ROW_D + 32 : ROWS] = jnp.zeros((ROWS - ROW_D - 32, 256), BF16)


def step_kernel(
    sizes, groups, plans, owners, camera, ray_mask, direction, target, levels, bins, anchors,
    encoder, middle, viewer, colour, scalars, result,
    enc, h1, h2, hv, raw, tints, depth, weight, passed, back, hist, w_e, w_m, w_mt, w_v, w_vt, w_c, w_ct, bias, per_ray,
    g_e, g_m, g_v, g_c, g_r, mine, halo, send, recv, *sums,
):
    tile_rows, tile_cols = camera.shape
    lanes = tile_rows * tile_cols
    cameras = anchors.shape[1]
    points = CHUNK * lanes
    per_chunk = CHUNK // GROUP
    tx, ty = lax.axis_index("tx"), lax.axis_index("ty")
    device = tx * sizes["ty"] + ty
    sides = (
        ({"tx": tx - 1}, tx > 0),
        ({"tx": tx + 1}, tx < sizes["tx"] - 1),
        ({"ty": ty - 1}, ty > 0),
        ({"ty": ty + 1}, ty < sizes["ty"] - 1),
    )
    sum_of = []
    at = 0
    for plan, least in plans:
        length = 4 + 2 * len(plan)
        sum_of.append(Sum(plan, least, sums[at : at + length]))
        at += length
    params, params_fine, grads, grads_fine, counting = sum_of

    choose_e = selector(64, encoder.shape[0], LPOS, 32, BF16)
    choose_d = selector(32, viewer.shape[0] - 256, LDIR, 16, BF16)
    trees = (encoder, middle, viewer, colour, scalars)
    for net, where in ((0, params), (1, params_fine)):
        owned = [owners[net, group] == device for group in range(5)]
        pack(owned, net, choose_e, choose_d, where.source, *trees)

    tall = jnp.concatenate(
        [direction[k] for k in range(3)]
        + [target[k] for k in range(3)]
        + [ray_mask[...].astype(F32), camera[...].astype(F32)],
        0,
    )
    repeat = (iota((tile_cols, lanes), 1) % tile_cols == iota((tile_cols, lanes), 0)).astype(F32)
    wide = dot(tall, repeat, HIGH)
    keep = iota((tile_rows, lanes), 1) // tile_cols == iota((tile_rows, lanes), 0)
    rows = [
        jnp.sum(jnp.where(keep, wide[k * tile_rows : k * tile_rows + tile_rows], 0.0), 0, keepdims=True)
        for k in range(8)
    ]
    mask, camera_row = rows[6], rows[7]
    target_rows = rows[3:6]
    number = iota((128, lanes), 0)
    picks = camera_row == number.astype(F32)
    counting.source[...] = dot_nt(
        jnp.broadcast_to(mask, (8, lanes)).astype(BF16), (picks | (number == 127)).astype(BF16)
    )
    picks = picks.astype(F32)
    greet(groups, sides[:2])
    params.step(0)
    counting.step(0)

    centres = jnp.concatenate([anchors[...], jnp.zeros((3, 128 - cameras), F32)], 1)
    origin = dot(centres, picks, HIGH)
    basis = jnp.concatenate([origin] + rows[0:3] + [jnp.zeros((2, lanes), F32)], 0)
    row8 = iota((8, lanes), 0)
    row32 = iota((32, lanes), 0)
    lift = iota((40, 8), 0)
    third = jnp.where(lift < 32, lift % 3, jnp.where(lift == 38, 2, -9))
    o_all = dot((third == iota((40, 8), 1)).astype(F32), basis, HIGH)
    d_all = dot((third + 3 == iota((40, 8), 1)).astype(F32), basis, HIGH)
    o_main, d_main = o_all[:32], d_all[:32]
    o_last, d_last = jnp.where(row8 == 7, 1.0 / shrink, o_all[32:]), d_all[32:]
    half_pi = jnp.float32(math.pi) * 0.5
    scale = jnp.zeros((32, lanes), F32)
    for level in range(LPOS):
        scale = jnp.where((row32 >= 3 * level) & (row32 < 3 * level + 3), half_pi * (2.0**level), scale)

    row16 = iota((16, lanes), 0)
    scale_d = scale[:16]
    sin_d, cos_d = sin_cos_twice(d_main[:16] * scale_d)
    top = jnp.where(row16 >= 12, jnp.where(row16 < 15, d_main[:16], 0.0), sin_d)
    bottom = jnp.where(row16 >= 12, jnp.where(row16 == 12, 1.0, 0.0), cos_d)
    view_code = jnp.concatenate([top, bottom], 0).astype(BF16)

    samples_fine = levels.shape[1]
    blocks_of = (SC // GROUP, samples_fine // GROUP)
    first_block = (0, blocks_of[0])
    for b in range(blocks_of[0]):
        depth[b] = near_plane + (far_plane - near_plane) * ((row8 + b * GROUP).astype(F32) + 0.5) / SC
    turned = levels[...].astype(F32).T
    for b in range(blocks_of[1]):
        at = turned[b * GROUP : b * GROUP + GROUP]
        depth[blocks_of[0] + b] = near_plane + (far_plane - near_plane) * (at + 0.5) / NT
    bins_turned = bins[...].astype(F32).T

    def encode(b, carry):
        for s in range(GROUP):
            t = depth[b, s : s + 1]
            place = (o_main + t * d_main) * shrink
            wave, cowave = sin_cos_twice(place * scale)
            wave = jnp.where(row32 >= 30, place, wave)
            extra = (o_last + t * d_last) * shrink
            end = jnp.where(row8 >= 6, extra, cowave[24:])
            cowave = jnp.concatenate([cowave[:24], end], 0)
            enc[b, 0:32, s * lanes : s * lanes + lanes] = wave.astype(BF16)
            enc[b, 32:64, s * lanes : s * lanes + lanes] = cowave.astype(BF16)
        return carry

    all_blocks = sum(blocks_of)
    cuts = [all_blocks * k // (params.steps - 1) for k in range(params.steps)]
    for k in range(1, params.steps):
        lax.fori_loop(cuts[k - 1], cuts[k], encode, 0)
        params.step(k)
        if k < counting.steps:
            counting.step(k)

    count = counting.whole[...]
    mask_floor = jnp.maximum(count[0:1, 127:128], 1.0)
    inverse = 1.0 / jnp.maximum(count, 1.0)
    ray_weight = dot(inverse, picks, HIGH)[0:1] * mask / cameras
    ones = jnp.full((16, points), 1.0, BF16)
    loss = jnp.zeros((1, lanes), F32)

    chunks_of = [n // per_chunk for n in blocks_of]

    def spread_over(steps, over):
        return {steps[k]: (over * k) // len(steps) for k in range(len(steps))}

    half = params.steps // 2
    beside = {
        (0, "forward"): [(params_fine, spread_over(range(0, half - 1), chunks_of[0]))],
        (0, "backward"): [(params_fine, spread_over(range(half - 1, params.steps), chunks_of[0]))],
        (1, "forward"): [(grads, spread_over(range(0, half + 1), chunks_of[1]))],
        (1, "backward"): [(grads, spread_over(range(half + 1, grads.steps), chunks_of[1]))],
    }

    def send_on(net, name, c):
        for moved, spots in beside[(net, name)]:
            for k, spot in spots.items():

                @pl.when(c == spot)
                def _(moved=moved, k=k):
                    moved.step(k)

    for net in range(2):
        blocks, first, chunks = blocks_of[net], first_block[net], chunks_of[net]
        held = (params, params_fine)[net].whole
        middle_now = held[ROW_M : ROW_M + 256]
        w_m[...] = middle_now
        w_mt[...] = middle_now.astype(F32).T.astype(BF16)
        misc32 = held[ROW_S : ROW_S + 16].astype(F32)
        row = iota((16, 256), 0)
        views = held[ROW_V : ROW_V + 128]
        w_vt[0:128, 0:128] = views[:, 0:128]
        w_vt[128:256, 0:128] = views[:, 128:256]
        w_v[0:128, 0:128] = views[:, 0:128].astype(F32).T.astype(BF16)
        w_v[0:128, 128:256] = views[:, 128:256].astype(F32).T.astype(BF16)
        w_v[128:144] = jnp.where(row == 0, misc32, 0.0).astype(BF16)
        sigma_t = jnp.concatenate([jnp.zeros((3, 256), F32), misc32[0:1], jnp.zeros((124, 256), F32)], 0).T
        w_vt[:, 128:144] = sigma_t[:, :16].astype(BF16)
        w_e[...] = held[ROW_E : ROW_E + 64].astype(F32).T.astype(BF16)
        last = held[ROW_D : ROW_D + 32].astype(F32)
        paint = last[:16, 128:]
        tail = misc32[2:3]
        sigma_bias = tail[:, 0:1]
        lane = iota((16, 128), 1)
        row_c = iota((16, 128), 0)
        tint_bias = jnp.zeros((16, 128), F32)
        for k in range(3):
            tint_bias = jnp.where((row_c == k) & (lane == 0), tail[:, 129 + k : 130 + k], tint_bias)
        w_c[:, 0:128] = paint.astype(BF16)
        w_c[:, 128:144] = tint_bias[:, :16].astype(BF16)
        w_ct[...] = jnp.concatenate([paint, jnp.zeros((112, 128), F32)], 0).T[:, :16].astype(BF16)
        bias[...] = jnp.broadcast_to(misc32[1:2], (128, 256)).T
        views_d = last[:, :128]
        shifted = pltpu.roll(jnp.broadcast_to(tail, (8, 256)), 255, 1)[0:1, :128]
        views_d = jnp.where(iota((32, 128), 0) == 28, shifted, views_d)
        per_ray[...] = dot_tn(views_d.astype(BF16), view_code)

        def code_of(c):
            start = first + c * per_chunk
            return jnp.concatenate([enc[start + i] for i in range(per_chunk)], 1)

        def forward(c, carry):
            send_on(net, "forward", c)
            one = jnp.maximum(dot(w_e[...], code_of(c)).astype(BF16), 0)
            h1[c] = one
            two = dot(w_m[...], one) + jnp.tile(bias[...], (1, points // 128))
            two = jnp.maximum(two.astype(BF16), 0)
            h2[c] = two
            out = dot(w_v[...], two)
            view = out[:128] + jnp.tile(per_ray[...], (1, CHUNK))
            view = jnp.maximum(view.astype(BF16), 0)
            hv[c] = view
            paint = dot(w_c[...], jnp.concatenate([view, ones], 0))
            for s in range(CHUNK):
                part = slice(s * lanes, s * lanes + lanes)
                b, r = c * per_chunk + s // GROUP, s % GROUP
                for k in range(3):
                    raw[k, b, r : r + 1] = paint[k : k + 1, part]
                raw[3, b, r : r + 1] = out[128:129, part]
            return carry

        lax.fori_loop(0, chunks, forward, 0)

        before = jnp.zeros((1, lanes), F32)
        shade = [jnp.zeros((8, lanes), F32) for _ in range(3)]
        far, opaque = jnp.zeros((8, lanes), F32), jnp.zeros((8, lanes), F32)

        def spacing(b):
            t = depth[first + b]
            after = depth[first + b + 1, 0:1] if b + 1 < blocks else jnp.full((1, lanes), far_plane, F32)
            return jnp.where(row8 == 7, after, pltpu.roll(t, 7, 0)) - t

        for b in range(blocks):
            zs = raw[3, b] + sigma_bias
            density = jnp.maximum(zs, 0.0) + jnp.log1p(jnp.exp(-jnp.abs(zs)))
            q = density * spacing(b)
            inclusive = running(q) + before
            before = inclusive[7:8]
            lit = jnp.exp(-(inclusive - q))
            w = lit * (1.0 - jnp.exp(-q))
            weight[b] = w
            passed[b] = jnp.exp(-inclusive)
            if net == 1:
                back[3, b] = density * mask
            for k in range(3):
                tint = jax.nn.sigmoid(raw[k, b])
                tints[k, b] = tint
                shade[k] = shade[k] + w * tint
            far = far + w * depth[first + b]
            opaque = opaque + w
        shade = [total(x) for x in shade]
        far, opaque = total(far), total(opaque)
        miss = [shade[k] - target_rows[k] for k in range(3)]
        loss = loss + ray_weight * (miss[0] * miss[0] + miss[1] * miss[1] + miss[2] * miss[2])
        seed = [2.0 * ray_weight * miss[k] for k in range(3)]
        seed_depth = seed_opaque = None
        if net == 1:
            for k in range(3):
                mine[k : k + 1] = shade[k]
            mine[3:4] = far
            mine[4:5] = mask
            mine[5:8] = jnp.zeros((3, lanes), F32)

            def across(i, slot):
                return pltpu.make_async_remote_copy(
                    mine, halo.at[slot], send.at[i], recv.at[slot], device_id=sides[i][0], device_id_type=MESH
                )

            for i in range(4):
                pl.when(sides[i][1])(lambda i=i: across(i, i).start())

            def count_bin(b, carry):
                sums = jnp.zeros((8, lanes), F32)
                for s in range(blocks):
                    sums = sums + jnp.where(bins_turned[s * GROUP : s * GROUP + GROUP] == b.astype(F32), back[3, s], 0.0)
                hist[b] = sums
                return carry

            lax.fori_loop(0, NHIST, count_bin, 0)
            binned = dot_nt(jnp.full((8, lanes), 1.0, F32), jnp.sum(hist[...], 1), HIGH)[0:1] / mask_floor
            solid = 0.01 + 0.98 * opaque
            entropy = -mask * (solid * jnp.log(solid) + (1.0 - solid) * jnp.log(1.0 - solid))
            seed_opaque = -(entropy_weight / mask_floor) * mask * 0.98 * (jnp.log(solid) - jnp.log(1.0 - solid))
            for i in range(4):
                @pl.when(sides[i][1])
                def _(i=i):
                    across(i, i).wait_send()
                    across(i, i ^ 1).wait_recv()

            values = mine[...]
            lane = iota((8, lanes), 1)
            col, tile_row = lane % tile_cols, lane // tile_cols

            def beyond(i, inner, shift, wrap):
                other = jnp.where(
                    inner, pltpu.roll(values, shift % lanes, 1), pltpu.roll(halo[i ^ 1], wrap % lanes, 1)
                )
                return jnp.where(inner | sides[i][1], other, 0.0)

            smooth = jnp.zeros((8, lanes), F32)
            pull = jnp.zeros((8, lanes), F32)
            for i, inner, shift, wrap in (
                (0, col > 0, 1, 1 - tile_cols),
                (1, col < tile_cols - 1, -1, tile_cols - 1),
                (2, tile_row > 0, tile_cols, tile_cols - lanes),
                (3, tile_row < tile_rows - 1, -tile_cols, lanes - tile_cols),
            ):
                other = beyond(i, inner, shift, wrap)
                pair = other[4:5] * mask
                gap = jnp.where(row8 < 4, values - other, 0.0)
                pull = pull + pair * gap
                if i % 2 == 1:
                    smooth = smooth + pair * gap * gap
            pull = (2.0 * smooth_weight / mask_floor) * pull
            seed = [seed[k] + pull[k : k + 1] for k in range(3)]
            seed_depth = pull[3:4]
            loss = loss + (smooth_weight * total(smooth) + entropy_weight * entropy) / mask_floor

        later = jnp.zeros((1, lanes), F32)
        for b in reversed(range(blocks)):
            w = weight[b]
            tint = [tints[k, b] for k in range(3)]
            pulled = seed[0] * tint[0] + seed[1] * tint[1] + seed[2] * tint[2]
            if net == 1:
                pulled = pulled + seed_depth * depth[first + b] + seed_opaque
            weighted = pulled * w
            onward = running_back(weighted) + later
            later = onward[0:1]
            dq = pulled * passed[b] - (onward - weighted)
            back[3, b] = dq * spacing(b) * jax.nn.sigmoid(raw[3, b] + sigma_bias)
            for k in range(3):
                back[k, b] = w * seed[k] * tint[k] * (1.0 - tint[k])

        for ref in (g_e, g_m, g_v, g_c, g_r):
            ref[...] = jnp.zeros_like(ref)

        def backward(c, carry):
            send_on(net, "backward", c)
            parts = []
            for s in range(CHUNK):
                b, r = c * per_chunk + s // GROUP, s % GROUP
                parts.append(jnp.concatenate([back[k, b, r : r + 1] for k in range(4)] + [jnp.zeros((12, lanes), F32)], 0))
            gate = jnp.concatenate(parts, 1).astype(BF16)
            view = hv[c]
            gv = jnp.where(view > 0, dot(w_ct[...], gate).astype(BF16), 0)
            sums = g_r[...]
            for s in range(CHUNK):
                sums = sums + gv[:, s * lanes : s * lanes + lanes].astype(F32)
            g_r[...] = sums
            g_c[...] += dot_nt(gate, jnp.concatenate([view, ones], 0))
            both = jnp.concatenate([gv, gate], 0)
            two = h2[c]
            g_v[...] += dot_nt(both, two)
            g2 = jnp.where(two > 0, dot(w_vt[...], both).astype(BF16), 0)
            one = h1[c]
            g_m[...] += dot_nt(jnp.concatenate([one, ones], 0), g2)
            g1 = jnp.where(one > 0, dot(w_mt[...], g2).astype(BF16), 0)
            g_e[...] += dot_nt(code_of(c), g1)
            return carry

        lax.fori_loop(0, chunks, backward, 0)

        out = (grads, grads_fine)[net].source
        out[ROW_M : ROW_M + 256] = g_m[0:256]
        out[ROW_V : ROW_V + 128] = g_v[0:128]
        lane = iota((16, 256), 1)
        grad_misc = jnp.where(row == 0, g_v[131:132], jnp.where(row == 1, g_m[256:257], 0.0))
        sums_c = g_c[:, 128:129]
        for k, spot in ((3, 0), (0, 129), (1, 130), (2, 131)):
            grad_misc = jnp.where((row == 2) & (lane == spot), sums_c[k : k + 1], grad_misc)
        out[ROW_S : ROW_S + 16] = grad_misc
        out[ROW_E : ROW_E + 64] = g_e[...]
        out[ROW_D : ROW_D + 32, 0:128] = dot_nt(view_code.astype(F32), g_r[...], HIGH)
        out[ROW_D : ROW_D + 32, 128:256] = jnp.concatenate([g_c[:, :128], jnp.zeros((16, 128), F32)], 0)
        out[ROW_D + 32 : ROWS] = jnp.zeros((ROWS - ROW_D - 32, 256), F32)
    last_rows = grads_fine.source
    last_rows[ROW_D + 32 : ROW_D + 33, 0:NHIST] = binned
    fold = loss[:, :128]
    for k in range(1, lanes // 128):
        fold = fold + loss[:, k * 128 : k * 128 + 128]
    last_rows[ROW_D + 33 : ROW_D + 34, 0:128] = fold
    for k in range(grads_fine.steps):
        grads_fine.step(k)
    result[0:ROWS] = grads.whole[...]
    result[ROWS : 2 * ROWS] = grads_fine.whole[...]


def adamw_update(weight, moment, square, gradient):
    moment_next = beta_first * moment + (1.0 - beta_first) * gradient
    square_next = beta_second * square + (1.0 - beta_second) * gradient * gradient
    first_hat = moment_next / (1.0 - beta_first**step_count)
    second_hat = square_next / (1.0 - beta_second**step_count)
    weight_next = weight - learn_rate * (
        first_hat / (jnp.sqrt(second_hat) + adam_epsilon) + decay_rate * weight
    )
    return (weight_next, moment_next, square_next)


def update_kernel(tiles_y, owners, grads, *refs):
    masters, moments, squares = refs[0:5], refs[5:10], refs[10:15]
    loss, histogram = refs[15], refs[16]
    nexts, next_moments, next_squares = refs[17:22], refs[22:27], refs[27:32]
    device = lax.axis_index("tx") * tiles_y + lax.axis_index("ty")
    histogram[...] = grads[ROWS + ROW_D + 32 : ROWS + ROW_D + 33, 0:NHIST]
    loss[...] = jnp.sum(grads[ROWS + ROW_D + 33 : ROWS + ROW_D + 34, 0:128], 1, keepdims=True)
    choose_e = selector(64, masters[0].shape[0], LPOS, 32, F32)
    choose_d = selector(32, masters[2].shape[0] - 256, LDIR, 16, F32)

    def step(group, net, at, gradient):
        owned = owners[net, group] == device
        old = [ref[at] for ref in (masters[group], moments[group], squares[group])]
        new = adamw_update(*old, gradient)
        for ref, was, now in zip((nexts[group], next_moments[group], next_squares[group]), old, new):
            ref[at] = jnp.where(owned, now, was)

    every = slice(None)
    for net in range(2):
        base = net * ROWS
        step(0, net, (every, net, every), dot_tn(choose_e, grads[base + ROW_E : base + ROW_E + 64], HIGH))
        step(1, net, (net,), grads[base + ROW_M : base + ROW_M + 256].T)
        views = grads[base + ROW_V : base + ROW_V + 128]
        step(2, net, (slice(0, 128), net, every), views[:, 0:128].T)
        step(2, net, (slice(128, 256), net, every), views[:, 128:256].T)
        last = grads[base + ROW_D : base + ROW_D + 32]
        rest = slice(256, masters[2].shape[0])
        step(2, net, (rest, net, every), dot_tn(choose_d, last[:, :128], HIGH))
        step(3, net, (every, net, every), last[0:3, 128:])
        misc = grads[base + ROW_S : base + ROW_S + 16]
        spot = slice(net, net + 1)
        step(4, net, (spot, slice(0, 256)), grads[base + ROW_E + 63 : base + ROW_E + 64])
        step(4, net, (spot, slice(256, 512)), misc[1:2])
        step(4, net, (spot, slice(512, 768)), misc[0:1])
        bias = jnp.concatenate([last[28:29, :128], jnp.zeros((1, 128), F32)], 1)
        bias = pltpu.roll(jnp.broadcast_to(bias, (8, 256)), 1, 1)[0:1]
        step(4, net, (spot, slice(768, 900)), (misc[2:3] + bias)[:, :132])


VMEM_SPEC = pl.BlockSpec(memory_space=pltpu.VMEM)
SMEM_SPEC = pl.BlockSpec(memory_space=pltpu.SMEM)


def per_device(sizes, camera, ray_mask, ray_direction, anchors, target, fine_levels, density_bins, owners, *trees):
    turns = ((2, 0, 1), (0, 1, 2), (2, 0, 1), (1, 0, 2), (0, 1))
    states = [jnp.transpose(x[0], turns[i % 5]) for i, x in enumerate(trees)]
    lanes = camera.shape[0] * camera.shape[1]
    samples = fine_levels.shape[0]
    levels = jnp.transpose(fine_levels, (1, 2, 0)).reshape(lanes, samples)
    bins = jnp.transpose(density_bins, (1, 2, 0)).reshape(lanes, samples)

    groups = groups_of(sizes)
    plans = [(plan_of(groups, ROWS, 16), 16)] * 2 + [(plan_of(groups, ROWS, 8), 8)] * 2 + [(plan_of(groups, 8, 16), 8)]
    sums = []
    for (plan, _), dtype, width in zip(plans, (BF16, BF16, F32, F32, F32), (256, 256, 256, 256, 128)):
        sums += sum_scratch(plan, dtype, width)
    points = CHUNK * lanes
    chunks = samples // CHUNK
    blocks = samples // GROUP
    grads = pl.pallas_call(
        functools.partial(step_kernel, sizes, groups, plans),
        out_shape=jax.ShapeDtypeStruct((2 * ROWS, 256), F32),
        in_specs=[SMEM_SPEC] + [VMEM_SPEC] * 12,
        out_specs=VMEM_SPEC,
        scratch_shapes=[
            pltpu.VMEM((blocks + SC // GROUP, 64, GROUP * lanes), BF16),
            pltpu.VMEM((chunks, 256, points), BF16),
            pltpu.VMEM((chunks, 256, points), BF16),
            pltpu.VMEM((chunks, 128, points), BF16),
            pltpu.VMEM((4, blocks, GROUP, lanes), F32),
            pltpu.VMEM((3, blocks, GROUP, lanes), F32),
            pltpu.VMEM((blocks + SC // GROUP, GROUP, lanes), F32),
            pltpu.VMEM((blocks, GROUP, lanes), F32),
            pltpu.VMEM((blocks, GROUP, lanes), F32),
            pltpu.VMEM((4, blocks, GROUP, lanes), F32),
            pltpu.VMEM((NHIST, 8, lanes), F32),
            pltpu.VMEM((256, 64), BF16),
            pltpu.VMEM((256, 256), BF16),
            pltpu.VMEM((256, 256), BF16),
            pltpu.VMEM((144, 256), BF16),
            pltpu.VMEM((256, 144), BF16),
            pltpu.VMEM((16, 144), BF16),
            pltpu.VMEM((128, 16), BF16),
            pltpu.VMEM((256, 128), F32),
            pltpu.VMEM((128, lanes), F32),
            pltpu.VMEM((64, 256), F32),
            pltpu.VMEM((272, 256), F32),
            pltpu.VMEM((144, 256), F32),
            pltpu.VMEM((16, 144), F32),
            pltpu.VMEM((128, lanes), F32),
            pltpu.VMEM((8, lanes), F32),
            pltpu.VMEM((4, 8, lanes), F32),
            pltpu.SemaphoreType.DMA((4,)),
            pltpu.SemaphoreType.DMA((4,)),
        ]
        + sums,
        compiler_params=pltpu.CompilerParams(collective_id=0, has_side_effects=True, vmem_limit_bytes=LIMIT),
        name="step",
    )(owners.T, camera, ray_mask, ray_direction, target, levels, bins, anchors, *states[:5])

    results = pl.pallas_call(
        functools.partial(update_kernel, sizes["ty"]),
        out_shape=[jax.ShapeDtypeStruct((1, 1), F32), jax.ShapeDtypeStruct((1, NHIST), F32)]
        + [jax.ShapeDtypeStruct(x.shape, F32) for x in states],
        in_specs=[SMEM_SPEC] + [VMEM_SPEC] * 16,
        out_specs=[VMEM_SPEC] * 17,
        name="update",
    )(owners.T, grads, *states)
    turned = []
    for i, x in enumerate(results[2:]):
        turn = turns[i % 5]
        turned.append(jnp.transpose(x, [turn.index(d) for d in range(len(turn))])[None])
    return (results[0].reshape(()), results[1].reshape(NHIST)) + tuple(turned)


def solution(mesh):
    sizes = dict(mesh.shape)
    tiled, tiled3 = P("ty", "tx"), P(None, "ty", "tx")
    slots = P(("tx", "ty"), None, None, None)
    trees = (slots, slots, slots, slots, P(("tx", "ty"), None, None))
    return jax.shard_map(
        functools.partial(per_device, sizes),
        mesh=mesh,
        in_specs=(tiled, tiled, tiled3, P(), tiled3, tiled3, tiled3, P()) + trees * 3,
        out_specs=(P(), P()) + trees * 3,
        check_vma=False,
    )
```

time: 201 us -> 137 us (0.68)
  Pallas kernels: 173 us -> 136 us
  local copies, waits for them, and re-layouts: 24.2 us -> 0 us
    pallas_call x3 -> x1, Pallas kernels: 168 us -> 130 us  [per_device(): pl.pallas_call(functools.partial(step_kernel, sizes, groups, plans), out_...]
    unnamed x65 -> x0, local copies, waits for them, and re-layouts: 17.6 us -> none
    reshape x4 -> x0, local copies, waits for them, and re-layouts: 2.41 us -> none  [the longest x1 0.82 us: per_device(): direction = ray_direction.reshape(3, lanes)]
where the time goes in v2:
time: 137 us
  Pallas kernels  136 us (99%)
    pallas_call x1, Pallas kernels, per_device(): pl.pallas_call(functools.partial(step_kernel, sizes, groups, plans), out_...  130 us
    pallas_call x1, Pallas kernels, per_device(): pl.pallas_call(functools.partial(update_kernel, sizes['ty']), out_shape=[...  6.65 us

profile of v2, /device:TPU:0, one launch (start us, length us, event | category | flops | bytes accessed | tf_op | source)
XLA Modules:
  0.0 137.3 jit_solution(6258189681454311665)
XLA Ops:
  0.7 129.8 %step.1.grads = f32[1024,256]{1,0:T(8,128)} custom-call(s32[2,5]{1,0:T(2,128)} %bitcast.95, s32[16,16]{1,0:T(8,128)} %camera.1, s32[16,16]{1,0:T(8,128)} %ray_mask.1, f32[3,16,16]{2,1,0:T(8,128)} %direction.1, f32[3,16,16]{2,1,0:T(8,128)} %target.1, s32[256,128]{1,0:T(8,128)} %bitcast.85, s32[256,128]{1,0:T(8,128)} %bitcast.86, f32[3,100]{1,0:T(4,128)} %anchors.1, ...), custom_call_target="tpu_custom_call" | custom-call | tf_op jit(solution)/shard_map/step/pallas_call | solution.py:713
  130.5 6.6 %update.1 = (f32[1,1]{1,0:T(1,128)}, f32[1,64]{1,0:T(1,128)}, f32[63,2,256]{2,1,0:T(2,128)}, f32[2,256,256]{2,1,0:T(8,128)}, f32[283,2,128]{2,1,0:T(2,128)}, /*i...) custom-call(s32[2,5]{1,0:T(2,128)} %bitcast.96, ...), custom_call_target="tpu_custom_call" | custom-call | tf_op jit(solution)/shard_map/update/pallas_call | solution.py:754

commit v3 on v2

--- a/solution.py
+++ b/solution.py
@@ -31,9 +31,10 @@
 BF16 = jnp.bfloat16
 HIGH = lax.Precision.HIGHEST
 GROUP = 8
-CHUNK = 8
+CHUNK = 16
 ROWS = 512
-LIMIT = 66_000_000
+LIMIT = 67_000_000
+PACE = (0, 0, 7, 19, 19, 24, 24)
 
 ROW_M, ROW_V, ROW_S, ROW_E, ROW_D = 0, 256, 384, 400, 464
 
@@ -104,10 +105,10 @@
     return [g for g in groups if g.count > 1]
 
 
-def plan_of(groups, rows, least):
+def plan_of(groups, rows, least, whole=()):
     plan = []
     for group in groups:
-        after = rows // group.count if rows % (group.count * least) == 0 else rows
+        after = rows // group.count if rows % (group.count * least) == 0 and group not in whole else rows
         plan.append((group, rows, after))
         rows = after
     return plan
@@ -230,7 +231,7 @@
         def _(where=where):
             pl.semaphore_signal(barrier, inc=1, device_id=where, device_id_type=MESH)
 
-    pl.semaphore_wait(barrier, expected)
+    return expected
 
 
 def running(block):
@@ -276,8 +277,8 @@
 def step_kernel(
     sizes, groups, plans, owners, camera, ray_mask, direction, target, levels, bins, anchors,
     encoder, middle, viewer, colour, scalars, result,
-    enc, h1, h2, hv, raw, tints, depth, weight, passed, back, hist, w_e, w_m, w_mt, w_v, w_vt, w_c, w_ct, bias, per_ray,
-    g_e, g_m, g_v, g_c, g_r, mine, halo, send, recv, *sums,
+    enc, h1, h2, hv, raw, depth, weight, passed, back, hist, w_e, w_m, w_mt, w_v, w_vt, w_c, w_ct, bias, per_ray,
+    g_e, g_m, g_v, g_c, g_r, turned, mine, halo, send, recv, *sums,
 ):
     tile_rows, tile_cols = camera.shape
     lanes = tile_rows * tile_cols
@@ -298,14 +299,17 @@
         length = 4 + 2 * len(plan)
         sum_of.append(Sum(plan, least, sums[at : at + length]))
         at += length
-    params, params_fine, grads, grads_fine, counting = sum_of
+    params, params_fine, counting = sum_of[:3]
+    grads, grads_fine = sum_of[3:5], sum_of[5:7]
+    expected = greet(groups, sides[:2])
 
     choose_e = selector(64, encoder.shape[0], LPOS, 32, BF16)
     choose_d = selector(32, viewer.shape[0] - 256, LDIR, 16, BF16)
     trees = (encoder, middle, viewer, colour, scalars)
-    for net, where in ((0, params), (1, params_fine)):
-        owned = [owners[net, group] == device for group in range(5)]
-        pack(owned, net, choose_e, choose_d, where.source, *trees)
+    owned = [[owners[net, group] == device for group in range(5)] for net in range(2)]
+    pack(owned[0], 0, choose_e, choose_d, params.source, *trees)
+    pl.semaphore_wait(pltpu.get_barrier_semaphore(), expected)
+    params.step(0)
 
     tall = jnp.concatenate(
         [direction[k] for k in range(3)]
@@ -328,9 +332,8 @@
         jnp.broadcast_to(mask, (8, lanes)).astype(BF16), (picks | (number == 127)).astype(BF16)
     )
     picks = picks.astype(F32)
-    greet(groups, sides[:2])
-    params.step(0)
     counting.step(0)
+    pack(owned[1], 1, choose_e, choose_d, params_fine.source, *trees)
 
     centres = jnp.concatenate([anchors[...], jnp.zeros((3, 128 - cameras), F32)], 1)
     origin = dot(centres, picks, HIGH)
@@ -360,9 +363,9 @@
     first_block = (0, blocks_of[0])
     for b in range(blocks_of[0]):
         depth[b] = near_plane + (far_plane - near_plane) * ((row8 + b * GROUP).astype(F32) + 0.5) / SC
-    turned = levels[...].astype(F32).T
+    levels_turned = levels[...].astype(F32).T
     for b in range(blocks_of[1]):
-        at = turned[b * GROUP : b * GROUP + GROUP]
+        at = levels_turned[b * GROUP : b * GROUP + GROUP]
         depth[blocks_of[0] + b] = near_plane + (far_plane - near_plane) * (at + 0.5) / NT
     bins_turned = bins[...].astype(F32).T
 
@@ -380,9 +383,12 @@
         return carry
 
     all_blocks = sum(blocks_of)
-    cuts = [all_blocks * k // (params.steps - 1) for k in range(params.steps)]
+    done = 0
     for k in range(1, params.steps):
-        lax.fori_loop(cuts[k - 1], cuts[k], encode, 0)
+        until = all_blocks * PACE[min(k, len(PACE) - 1)] // PACE[-1]
+        if until > done:
+            lax.fori_loop(done, until, encode, 0)
+        done = until
         params.step(k)
         if k < counting.steps:
             counting.step(k)
@@ -396,24 +402,25 @@
 
     chunks_of = [n // per_chunk for n in blocks_of]
 
-    def spread_over(steps, over):
-        return {steps[k]: (over * k) // len(steps) for k in range(len(steps))}
+    def at_chunks(moved, pairs, over):
+        return [(part, k, over * eighth // 8) for k, eighth in pairs for part in moved]
 
     half = params.steps // 2
     beside = {
-        (0, "forward"): [(params_fine, spread_over(range(0, half - 1), chunks_of[0]))],
-        (0, "backward"): [(params_fine, spread_over(range(half - 1, params.steps), chunks_of[0]))],
-        (1, "forward"): [(grads, spread_over(range(0, half + 1), chunks_of[1]))],
-        (1, "backward"): [(grads, spread_over(range(half + 1, grads.steps), chunks_of[1]))],
+        (0, "forward"): at_chunks([params_fine], [(0, 0), (1, 2), (2, 6)][:half], chunks_of[0]),
+        (0, "backward"): at_chunks([params_fine], [(k, min(2 + 4 * (k > half + 1), 6)) for k in range(half, params.steps - 1)], chunks_of[0]),
+        (1, "forward"): at_chunks(grads, [(0, 0), (1, 1), (2, 4), (3, 7)][: half + 1], chunks_of[1]),
+        (1, "backward"): at_chunks(grads, [(k, min(1 + 2 * (k - half - 1), 7)) for k in range(half + 1, params.steps)], chunks_of[1]),
     }
 
     def send_on(net, name, c):
-        for moved, spots in beside[(net, name)]:
-            for k, spot in spots.items():
-
-                @pl.when(c == spot)
-                def _(moved=moved, k=k):
-                    moved.step(k)
+        for spot in sorted({spot for _, _, spot in beside[(net, name)]}):
+
+            @pl.when(c == spot)
+            def _(spot=spot):
+                for moved, k, where in beside[(net, name)]:
+                    if where == spot:
+                        moved.step(k)
 
     for net in range(2):
         blocks, first, chunks = blocks_of[net], first_block[net], chunks_of[net]
@@ -499,7 +506,7 @@
                 back[3, b] = density * mask
             for k in range(3):
                 tint = jax.nn.sigmoid(raw[k, b])
-                tints[k, b] = tint
+                raw[k, b] = tint
                 shade[k] = shade[k] + w * tint
             far = far + w * depth[first + b]
             opaque = opaque + w
@@ -528,11 +535,13 @@
                 sums = jnp.zeros((8, lanes), F32)
                 for s in range(blocks):
                     sums = sums + jnp.where(bins_turned[s * GROUP : s * GROUP + GROUP] == b.astype(F32), back[3, s], 0.0)
-                hist[b] = sums
+                hist[b] = sums[:, :128]
+                for k in range(1, lanes // 128):
+                    hist[b] += sums[:, k * 128 : k * 128 + 128]
                 return carry
 
             lax.fori_loop(0, NHIST, count_bin, 0)
-            binned = dot_nt(jnp.full((8, lanes), 1.0, F32), jnp.sum(hist[...], 1), HIGH)[0:1] / mask_floor
+            binned = dot_nt(jnp.full((8, 128), 1.0, F32), jnp.sum(hist[...], 1), HIGH)[0:1] / mask_floor
             solid = 0.01 + 0.98 * opaque
             entropy = -mask * (solid * jnp.log(solid) + (1.0 - solid) * jnp.log(1.0 - solid))
             seed_opaque = -(entropy_weight / mask_floor) * mask * 0.98 * (jnp.log(solid) - jnp.log(1.0 - solid))
@@ -574,7 +583,7 @@
         later = jnp.zeros((1, lanes), F32)
         for b in reversed(range(blocks)):
             w = weight[b]
-            tint = [tints[k, b] for k in range(3)]
+            tint = [raw[k, b] for k in range(3)]
             pulled = seed[0] * tint[0] + seed[1] * tint[1] + seed[2] * tint[2]
             if net == 1:
                 pulled = pulled + seed_depth * depth[first + b] + seed_opaque
@@ -602,42 +611,48 @@
             for s in range(CHUNK):
                 sums = sums + gv[:, s * lanes : s * lanes + lanes].astype(F32)
             g_r[...] = sums
-            g_c[...] += dot_nt(gate, jnp.concatenate([view, ones], 0))
+            g_c[...] += dot_nt(jnp.concatenate([view, ones], 0), gate)
             both = jnp.concatenate([gv, gate], 0)
             two = h2[c]
-            g_v[...] += dot_nt(both, two)
+            turned[...] = two.T
+            g_v[...] += dot(both, turned[...])
             g2 = jnp.where(two > 0, dot(w_vt[...], both).astype(BF16), 0)
             one = h1[c]
             g_m[...] += dot_nt(jnp.concatenate([one, ones], 0), g2)
             g1 = jnp.where(one > 0, dot(w_mt[...], g2).astype(BF16), 0)
-            g_e[...] += dot_nt(code_of(c), g1)
+            turned[...] = g1.T
+            g_e[...] += dot(code_of(c), turned[...])
             return carry
 
         lax.fori_loop(0, chunks, backward, 0)
-
-        out = (grads, grads_fine)[net].source
-        out[ROW_M : ROW_M + 256] = g_m[0:256]
-        out[ROW_V : ROW_V + 128] = g_v[0:128]
+        if net == 0:
+            params_fine.step(params.steps - 1)
+
+        tints = jnp.concatenate([g_c[...], jnp.zeros((144, 112), F32)], 1)
+        tints, sums_c = tints[:128].T[:16], tints[128:136].T[:16, 0:1]
+        upper, lower = [part.source for part in (grads, grads_fine)[net]]
+        upper[...] = g_m[0:256]
+        lower[ROW_V - 256 : ROW_V - 128] = g_v[0:128]
         lane = iota((16, 256), 1)
         grad_misc = jnp.where(row == 0, g_v[131:132], jnp.where(row == 1, g_m[256:257], 0.0))
-        sums_c = g_c[:, 128:129]
         for k, spot in ((3, 0), (0, 129), (1, 130), (2, 131)):
             grad_misc = jnp.where((row == 2) & (lane == spot), sums_c[k : k + 1], grad_misc)
-        out[ROW_S : ROW_S + 16] = grad_misc
-        out[ROW_E : ROW_E + 64] = g_e[...]
-        out[ROW_D : ROW_D + 32, 0:128] = dot_nt(view_code.astype(F32), g_r[...], HIGH)
-        out[ROW_D : ROW_D + 32, 128:256] = jnp.concatenate([g_c[:, :128], jnp.zeros((16, 128), F32)], 0)
-        out[ROW_D + 32 : ROWS] = jnp.zeros((ROWS - ROW_D - 32, 256), F32)
-    last_rows = grads_fine.source
-    last_rows[ROW_D + 32 : ROW_D + 33, 0:NHIST] = binned
+        lower[ROW_S - 256 : ROW_S - 240] = grad_misc
+        lower[ROW_E - 256 : ROW_E - 192] = g_e[...]
+        lower[ROW_D - 256 : ROW_D - 224, 0:128] = dot_nt(view_code.astype(F32), g_r[...], HIGH)
+        lower[ROW_D - 256 : ROW_D - 224, 128:256] = jnp.concatenate([tints, jnp.zeros((16, 128), F32)], 0)
+        lower[ROW_D - 224 : ROWS - 256] = jnp.zeros((ROWS - ROW_D - 32, 256), F32)
+    rest = grads_fine[1].source
+    rest[ROW_D - 224 : ROW_D - 223, 0:NHIST] = binned
     fold = loss[:, :128]
     for k in range(1, lanes // 128):
         fold = fold + loss[:, k * 128 : k * 128 + 128]
-    last_rows[ROW_D + 33 : ROW_D + 34, 0:128] = fold
-    for k in range(grads_fine.steps):
-        grads_fine.step(k)
-    result[0:ROWS] = grads.whole[...]
-    result[ROWS : 2 * ROWS] = grads_fine.whole[...]
+    rest[ROW_D - 223 : ROW_D - 222, 0:128] = fold
+    for k in range(params.steps):
+        for part in grads_fine:
+            part.step(k)
+    for i, part in enumerate(grads + grads_fine):
+        result[i * 256 : i * 256 + 256] = part.whole[...]
 
 
 def adamw_update(weight, moment, square, gradient):
@@ -652,44 +667,63 @@
 
 
 def update_kernel(tiles_y, owners, grads, *refs):
-    masters, moments, squares = refs[0:5], refs[5:10], refs[10:15]
-    loss, histogram = refs[15], refs[16]
-    nexts, next_moments, next_squares = refs[17:22], refs[22:27], refs[27:32]
+    given, loss, histogram, taken = refs[0:15], refs[15], refs[16], refs[17:32]
+    held, arrived, left = refs[32:47], refs[47], refs[48]
     device = lax.axis_index("tx") * tiles_y + lax.axis_index("ty")
+    order = (1, 2, 0, 4, 3)
+    for group in order:
+        for i in (group, group + 5, group + 10):
+            pltpu.make_async_copy(given[i], held[i], arrived.at[i]).start()
     histogram[...] = grads[ROWS + ROW_D + 32 : ROWS + ROW_D + 33, 0:NHIST]
     loss[...] = jnp.sum(grads[ROWS + ROW_D + 33 : ROWS + ROW_D + 34, 0:128], 1, keepdims=True)
-    choose_e = selector(64, masters[0].shape[0], LPOS, 32, F32)
-    choose_d = selector(32, masters[2].shape[0] - 256, LDIR, 16, F32)
-
-    def step(group, net, at, gradient):
-        owned = owners[net, group] == device
-        old = [ref[at] for ref in (masters[group], moments[group], squares[group])]
-        new = adamw_update(*old, gradient)
-        for ref, was, now in zip((nexts[group], next_moments[group], next_squares[group]), old, new):
-            ref[at] = jnp.where(owned, now, was)
+
+    def step(group, at, gradient):
+        trio = (held[group], held[group + 5], held[group + 10])
+        for ref, now in zip(trio, adamw_update(*[ref[at] for ref in trio], gradient)):
+            ref[at] = now
 
     every = slice(None)
-    for net in range(2):
+
+    def update(group, net):
         base = net * ROWS
-        step(0, net, (every, net, every), dot_tn(choose_e, grads[base + ROW_E : base + ROW_E + 64], HIGH))
-        step(1, net, (net,), grads[base + ROW_M : base + ROW_M + 256].T)
-        views = grads[base + ROW_V : base + ROW_V + 128]
-        step(2, net, (slice(0, 128), net, every), views[:, 0:128].T)
-        step(2, net, (slice(128, 256), net, every), views[:, 128:256].T)
         last = grads[base + ROW_D : base + ROW_D + 32]
-        rest = slice(256, masters[2].shape[0])
-        step(2, net, (rest, net, every), dot_tn(choose_d, last[:, :128], HIGH))
-        step(3, net, (every, net, every), last[0:3, 128:])
-        misc = grads[base + ROW_S : base + ROW_S + 16]
-        spot = slice(net, net + 1)
-        step(4, net, (spot, slice(0, 256)), grads[base + ROW_E + 63 : base + ROW_E + 64])
-        step(4, net, (spot, slice(256, 512)), misc[1:2])
-        step(4, net, (spot, slice(512, 768)), misc[0:1])
-        bias = jnp.concatenate([last[28:29, :128], jnp.zeros((1, 128), F32)], 1)
-        bias = pltpu.roll(jnp.broadcast_to(bias, (8, 256)), 1, 1)[0:1]
-        step(4, net, (spot, slice(768, 900)), (misc[2:3] + bias)[:, :132])
-
-
+        if group == 0:
+            choose = selector(64, held[0].shape[0], LPOS, 32, F32)
+            step(0, (every, net, every), dot_tn(choose, grads[base + ROW_E : base + ROW_E + 64], HIGH))
+        elif group == 1:
+            step(1, (net,), grads[base + ROW_M : base + ROW_M + 256].T)
+        elif group == 2:
+            views = grads[base + ROW_V : base + ROW_V + 128]
+            step(2, (slice(0, 128), net, every), views[:, 0:128].T)
+            step(2, (slice(128, 256), net, every), views[:, 128:256].T)
+            rest = slice(256, held[2].shape[0])
+            choose = selector(32, held[2].shape[0] - 256, LDIR, 16, F32)
+            step(2, (rest, net, every), dot_tn(choose, last[:, :128], HIGH))
+        elif group == 3:
+            step(3, (every, net, every), last[0:3, 128:])
+        else:
+            misc = grads[base + ROW_S : base + ROW_S + 16]
+            spot = slice(net, net + 1)
+            step(4, (spot, slice(0, 256)), grads[base + ROW_E + 63 : base + ROW_E + 64])
+            step(4, (spot, slice(256, 512)), misc[1:2])
+            step(4, (spot, slice(512, 768)), misc[0:1])
+            bias = jnp.concatenate([last[28:29, :128], jnp.zeros((1, 128), F32)], 1)
+            bias = pltpu.roll(jnp.broadcast_to(bias, (8, 256)), 1, 1)[0:1]
+            step(4, (spot, slice(768, 900)), (misc[2:3] + bias)[:, :132])
+
+    for group in order:
+        trio = (group, group + 5, group + 10)
+        for i in trio:
+            pltpu.make_async_copy(given[i], held[i], arrived.at[i]).wait()
+        for net in range(2):
+            pl.when(owners[net, group] == device)(functools.partial(update, group, net))
+        for i in trio:
+            pltpu.make_async_copy(held[i], taken[i], left.at[i]).start()
+    for i in range(15):
+        pltpu.make_async_copy(held[i], taken[i], left.at[i]).wait()
+
+
+ANY_SPEC = pl.BlockSpec(memory_space=pl.ANY)
 VMEM_SPEC = pl.BlockSpec(memory_space=pltpu.VMEM)
 SMEM_SPEC = pl.BlockSpec(memory_space=pltpu.SMEM)
 
@@ -703,9 +737,13 @@
     bins = jnp.transpose(density_bins, (1, 2, 0)).reshape(lanes, samples)
 
     groups = groups_of(sizes)
-    plans = [(plan_of(groups, ROWS, 16), 16)] * 2 + [(plan_of(groups, ROWS, 8), 8)] * 2 + [(plan_of(groups, 8, 16), 8)]
+    turned_round = groups[:1] + groups[:0:-1]
+    param_plan = plan_of(groups, ROWS, 16, groups[2:])
+    upper, lower = plan_of(groups, 256, 8), plan_of(turned_round, 256, 8)
+    plans = [(param_plan, 16), (param_plan, 16), (plan_of(groups, 8, 8, groups), 8)]
+    plans += [(upper, 8), (lower, 8)] * 2
     sums = []
-    for (plan, _), dtype, width in zip(plans, (BF16, BF16, F32, F32, F32), (256, 256, 256, 256, 128)):
+    for (plan, _), dtype, width in zip(plans, (BF16, BF16) + (F32,) * 5, (256, 256, 128) + (256,) * 4):
         sums += sum_scratch(plan, dtype, width)
     points = CHUNK * lanes
     chunks = samples // CHUNK
@@ -721,12 +759,11 @@
             pltpu.VMEM((chunks, 256, points), BF16),
             pltpu.VMEM((chunks, 128, points), BF16),
             pltpu.VMEM((4, blocks, GROUP, lanes), F32),
-            pltpu.VMEM((3, blocks, GROUP, lanes), F32),
             pltpu.VMEM((blocks + SC // GROUP, GROUP, lanes), F32),
             pltpu.VMEM((blocks, GROUP, lanes), F32),
             pltpu.VMEM((blocks, GROUP, lanes), F32),
             pltpu.VMEM((4, blocks, GROUP, lanes), F32),
-            pltpu.VMEM((NHIST, 8, lanes), F32),
+            pltpu.VMEM((NHIST, 8, 128), F32),
             pltpu.VMEM((256, 64), BF16),
             pltpu.VMEM((256, 256), BF16),
             pltpu.VMEM((256, 256), BF16),
@@ -739,8 +776,9 @@
             pltpu.VMEM((64, 256), F32),
             pltpu.VMEM((272, 256), F32),
             pltpu.VMEM((144, 256), F32),
-            pltpu.VMEM((16, 144), F32),
+            pltpu.VMEM((144, 16), F32),
             pltpu.VMEM((128, lanes), F32),
+            pltpu.VMEM((points, 256), BF16),
             pltpu.VMEM((8, lanes), F32),
             pltpu.VMEM((4, 8, lanes), F32),
             pltpu.SemaphoreType.DMA((4,)),
@@ -755,8 +793,10 @@
         functools.partial(update_kernel, sizes["ty"]),
         out_shape=[jax.ShapeDtypeStruct((1, 1), F32), jax.ShapeDtypeStruct((1, NHIST), F32)]
         + [jax.ShapeDtypeStruct(x.shape, F32) for x in states],
-        in_specs=[SMEM_SPEC] + [VMEM_SPEC] * 16,
-        out_specs=[VMEM_SPEC] * 17,
+        in_specs=[SMEM_SPEC, VMEM_SPEC] + [ANY_SPEC] * 15,
+        out_specs=[VMEM_SPEC] * 2 + [ANY_SPEC] * 15,
+        scratch_shapes=[pltpu.VMEM(x.shape, F32) for x in states]
+        + [pltpu.SemaphoreType.DMA((15,)), pltpu.SemaphoreType.DMA((15,))],
         name="update",
     )(owners.T, grads, *states)
     turned = []

time: 137 us -> 113 us (0.82)
  Pallas kernels: 136 us -> 112 us
    pallas_call x1, Pallas kernels: 130 us -> 107 us  [per_device(): pl.pallas_call(functools.partial(step_kernel, sizes, groups, plans), out_...]
where the time goes in v3:
time: 113 us
  Pallas kernels  112 us (99%)
    pallas_call x1, Pallas kernels, per_device(): pl.pallas_call(functools.partial(step_kernel, sizes, groups, plans), out_...  107 us
    pallas_call x1, Pallas kernels, per_device(): pl.pallas_call(functools.partial(update_kernel, sizes['ty']), out_shape=[...  5.56 us

profile of v3, /device:TPU:0, one launch (start us, length us, event | category | flops | bytes accessed | tf_op | source)
XLA Modules:
  0.0 113.3 jit_solution(14317341235102020744)
XLA Ops:
  0.7 106.9 %step.1.grads = f32[1024,256]{1,0:T(8,128)} custom-call(s32[2,5]{1,0:T(2,128)} %bitcast.95, s32[16,16]{1,0:T(8,128)} %camera.1, s32[16,16]{1,0:T(8,128)} %ray_mask.1, f32[3,16,16]{2,1,0:T(8,128)} %direction.1, f32[3,16,16]{2,1,0:T(8,128)} %target.1, s32[256,128]{1,0:T(8,128)} %bitcast.85, s32[256,128]{1,0:T(8,128)} %bitcast.86, f32[3,100]{1,0:T(4,128)} %anchors.1, ...), custom_call_target="tpu_custom_call" | custom-call | tf_op jit(solution)/shard_map/step/pallas_call | solution.py:751
  107.6 5.6 %update.1 = (f32[1,1]{1,0:T(1,128)}, f32[1,64]{1,0:T(1,128)}, f32[63,2,256]{2,1,0:T(2,128)}, f32[2,256,256]{2,1,0:T(8,128)}, f32[283,2,128]{2,1,0:T(2,128)}, /*i...) custom-call(s32[2,5]{1,0:T(2,128)} %bitcast.96, ...), custom_call_target="tpu_custom_call" | custom-call | tf_op jit(solution)/shard_map/update/pallas_call | solution.py:792

commit v4 on v3

--- a/solution.py
+++ b/solution.py
@@ -114,11 +114,11 @@
     return plan
 
 
-def sum_scratch(plan, dtype, width=256):
+def sum_scratch(plan, dtype, width, beyond):
     copies = sum(group.count - 1 for group, _, _ in plan)
     rows = plan[0][1]
     return (
-        [pltpu.VMEM((rows, width), dtype), pltpu.VMEM((rows, width), dtype)]
+        [pltpu.VMEM((rows + beyond, width), dtype), pltpu.VMEM((rows, width), dtype)]
         + [pltpu.VMEM((group.count, after, width), dtype) for group, _, after in plan]
         + [pltpu.VMEM((after, width), dtype) for _, _, after in plan]
         + [pltpu.SemaphoreType.DMA((2 * copies,)), pltpu.SemaphoreType.DMA((2 * copies,))]
@@ -277,9 +277,10 @@
 def step_kernel(
     sizes, groups, plans, owners, camera, ray_mask, direction, target, levels, bins, anchors,
     encoder, middle, viewer, colour, scalars, result,
-    enc, h1, h2, hv, raw, depth, weight, passed, back, hist, w_e, w_m, w_mt, w_v, w_vt, w_c, w_ct, bias, per_ray,
-    g_e, g_m, g_v, g_c, g_r, turned, mine, halo, send, recv, *sums,
+    enc, h1, h2, hv, raw, depth, back, hist, w_e, w_mt, w_v, w_vt, w_c, w_ct, bias, per_ray,
+    g_c, g_r, turned, mine, halo, send, recv, leaving, entering, *sums,
 ):
+    local, sums = sums[:7], sums[7:]
     tile_rows, tile_cols = camera.shape
     lanes = tile_rows * tile_cols
     cameras = anchors.shape[1]
@@ -302,6 +303,13 @@
     params, params_fine, counting = sum_of[:3]
     grads, grads_fine = sum_of[3:5], sum_of[5:7]
     expected = greet(groups, sides[:2])
+    given = (encoder, middle, viewer, colour, scalars, levels, bins)
+    inward = [pltpu.make_async_copy(x, here, entering.at[i]) for i, (x, here) in enumerate(zip(given, local))]
+    for copy in inward:
+        copy.start()
+    for copy in inward[:5]:
+        copy.wait()
+    encoder, middle, viewer, colour, scalars, levels, bins = local
 
     choose_e = selector(64, encoder.shape[0], LPOS, 32, BF16)
     choose_d = selector(32, viewer.shape[0] - 256, LDIR, 16, BF16)
@@ -358,6 +366,8 @@
     bottom = jnp.where(row16 >= 12, jnp.where(row16 == 12, 1.0, 0.0), cos_d)
     view_code = jnp.concatenate([top, bottom], 0).astype(BF16)
 
+    for copy in inward[5:]:
+        copy.wait()
     samples_fine = levels.shape[1]
     blocks_of = (SC // GROUP, samples_fine // GROUP)
     first_block = (0, blocks_of[0])
@@ -425,9 +435,7 @@
     for net in range(2):
         blocks, first, chunks = blocks_of[net], first_block[net], chunks_of[net]
         held = (params, params_fine)[net].whole
-        middle_now = held[ROW_M : ROW_M + 256]
-        w_m[...] = middle_now
-        w_mt[...] = middle_now.astype(F32).T.astype(BF16)
+        w_mt[...] = held[ROW_M : ROW_M + 256].astype(F32).T.astype(BF16)
         misc32 = held[ROW_S : ROW_S + 16].astype(F32)
         row = iota((16, 256), 0)
         views = held[ROW_V : ROW_V + 128]
@@ -465,7 +473,7 @@
             send_on(net, "forward", c)
             one = jnp.maximum(dot(w_e[...], code_of(c)).astype(BF16), 0)
             h1[c] = one
-            two = dot(w_m[...], one) + jnp.tile(bias[...], (1, points // 128))
+            two = dot(held[ROW_M : ROW_M + 256], one) + jnp.tile(bias[...], (1, points // 128))
             two = jnp.maximum(two.astype(BF16), 0)
             h2[c] = two
             out = dot(w_v[...], two)
@@ -500,8 +508,8 @@
             before = inclusive[7:8]
             lit = jnp.exp(-(inclusive - q))
             w = lit * (1.0 - jnp.exp(-q))
-            weight[b] = w
-            passed[b] = jnp.exp(-inclusive)
+            back[0, b] = w
+            back[1, b] = jnp.exp(-inclusive)
             if net == 1:
                 back[3, b] = density * mask
             for k in range(3):
@@ -535,9 +543,10 @@
                 sums = jnp.zeros((8, lanes), F32)
                 for s in range(blocks):
                     sums = sums + jnp.where(bins_turned[s * GROUP : s * GROUP + GROUP] == b.astype(F32), back[3, s], 0.0)
-                hist[b] = sums[:, :128]
+                folded = sums[:, :128]
                 for k in range(1, lanes // 128):
-                    hist[b] += sums[:, k * 128 : k * 128 + 128]
+                    folded = folded + sums[:, k * 128 : k * 128 + 128]
+                hist[b] = total(folded)
                 return carry
 
             lax.fori_loop(0, NHIST, count_bin, 0)
@@ -582,7 +591,7 @@
 
         later = jnp.zeros((1, lanes), F32)
         for b in reversed(range(blocks)):
-            w = weight[b]
+            w, passed = back[0, b], back[1, b]
             tint = [raw[k, b] for k in range(3)]
             pulled = seed[0] * tint[0] + seed[1] * tint[1] + seed[2] * tint[2]
             if net == 1:
@@ -590,12 +599,15 @@
             weighted = pulled * w
             onward = running_back(weighted) + later
             later = onward[0:1]
-            dq = pulled * passed[b] - (onward - weighted)
+            dq = pulled * passed - (onward - weighted)
             back[3, b] = dq * spacing(b) * jax.nn.sigmoid(raw[3, b] + sigma_bias)
             for k in range(3):
                 back[k, b] = w * seed[k] * tint[k] * (1.0 - tint[k])
 
-        for ref in (g_e, g_m, g_v, g_c, g_r):
+        upper, lower = [part.source for part in (grads, grads_fine)[net]]
+        g_m = upper
+        g_v, g_e = lower.at[ROW_V - 256 : ROW_V - 112], lower.at[ROW_E - 256 : ROW_E - 192]
+        for ref in (upper, lower, g_c, g_r):
             ref[...] = jnp.zeros_like(ref)
 
         def backward(c, carry):
@@ -630,18 +642,13 @@
 
         tints = jnp.concatenate([g_c[...], jnp.zeros((144, 112), F32)], 1)
         tints, sums_c = tints[:128].T[:16], tints[128:136].T[:16, 0:1]
-        upper, lower = [part.source for part in (grads, grads_fine)[net]]
-        upper[...] = g_m[0:256]
-        lower[ROW_V - 256 : ROW_V - 128] = g_v[0:128]
         lane = iota((16, 256), 1)
-        grad_misc = jnp.where(row == 0, g_v[131:132], jnp.where(row == 1, g_m[256:257], 0.0))
+        grad_misc = jnp.where(row == 0, lower[131:132], jnp.where(row == 1, upper[256:257], 0.0))
         for k, spot in ((3, 0), (0, 129), (1, 130), (2, 131)):
             grad_misc = jnp.where((row == 2) & (lane == spot), sums_c[k : k + 1], grad_misc)
         lower[ROW_S - 256 : ROW_S - 240] = grad_misc
-        lower[ROW_E - 256 : ROW_E - 192] = g_e[...]
         lower[ROW_D - 256 : ROW_D - 224, 0:128] = dot_nt(view_code.astype(F32), g_r[...], HIGH)
         lower[ROW_D - 256 : ROW_D - 224, 128:256] = jnp.concatenate([tints, jnp.zeros((16, 128), F32)], 0)
-        lower[ROW_D - 224 : ROWS - 256] = jnp.zeros((ROWS - ROW_D - 32, 256), F32)
     rest = grads_fine[1].source
     rest[ROW_D - 224 : ROW_D - 223, 0:NHIST] = binned
     fold = loss[:, :128]
@@ -651,8 +658,14 @@
     for k in range(params.steps):
         for part in grads_fine:
             part.step(k)
-    for i, part in enumerate(grads + grads_fine):
-        result[i * 256 : i * 256 + 256] = part.whole[...]
+    outward = [
+        pltpu.make_async_copy(part.whole, result.at[pl.ds(i * 256, 256)], leaving.at[i])
+        for i, part in enumerate(grads + grads_fine)
+    ]
+    for copy in outward:
+        copy.start()
+    for copy in outward:
+        copy.wait()
 
 
 def adamw_update(weight, moment, square, gradient):
@@ -739,20 +752,21 @@
     groups = groups_of(sizes)
     turned_round = groups[:1] + groups[:0:-1]
     param_plan = plan_of(groups, ROWS, 16, groups[2:])
-    upper, lower = plan_of(groups, 256, 8), plan_of(turned_round, 256, 8)
+    upper, lower = plan_of(groups, 256, 8, groups[2:]), plan_of(turned_round, 256, 8, turned_round[2:])
     plans = [(param_plan, 16), (param_plan, 16), (plan_of(groups, 8, 8, groups), 8)]
     plans += [(upper, 8), (lower, 8)] * 2
     sums = []
-    for (plan, _), dtype, width in zip(plans, (BF16, BF16) + (F32,) * 5, (256, 256, 128) + (256,) * 4):
-        sums += sum_scratch(plan, dtype, width)
+    kinds = [(BF16, 256, 0)] * 2 + [(F32, 128, 0)] + [(F32, 256, 16), (F32, 256, 0)] * 2
+    for (plan, _), kind in zip(plans, kinds):
+        sums += sum_scratch(plan, *kind)
     points = CHUNK * lanes
     chunks = samples // CHUNK
     blocks = samples // GROUP
     grads = pl.pallas_call(
         functools.partial(step_kernel, sizes, groups, plans),
         out_shape=jax.ShapeDtypeStruct((2 * ROWS, 256), F32),
-        in_specs=[SMEM_SPEC] + [VMEM_SPEC] * 12,
-        out_specs=VMEM_SPEC,
+        in_specs=[SMEM_SPEC] + [VMEM_SPEC] * 4 + [ANY_SPEC] * 2 + [VMEM_SPEC] + [ANY_SPEC] * 5,
+        out_specs=ANY_SPEC,
         scratch_shapes=[
             pltpu.VMEM((blocks + SC // GROUP, 64, GROUP * lanes), BF16),
             pltpu.VMEM((chunks, 256, points), BF16),
@@ -760,12 +774,9 @@
             pltpu.VMEM((chunks, 128, points), BF16),
             pltpu.VMEM((4, blocks, GROUP, lanes), F32),
             pltpu.VMEM((blocks + SC // GROUP, GROUP, lanes), F32),
-            pltpu.VMEM((blocks, GROUP, lanes), F32),
-            pltpu.VMEM((blocks, GROUP, lanes), F32),
             pltpu.VMEM((4, blocks, GROUP, lanes), F32),
-            pltpu.VMEM((NHIST, 8, 128), F32),
+            pltpu.VMEM((NHIST, 1, 128), F32),
             pltpu.VMEM((256, 64), BF16),
-            pltpu.VMEM((256, 256), BF16),
             pltpu.VMEM((256, 256), BF16),
             pltpu.VMEM((144, 256), BF16),
             pltpu.VMEM((256, 144), BF16),
@@ -773,9 +784,6 @@
             pltpu.VMEM((128, 16), BF16),
             pltpu.VMEM((256, 128), F32),
             pltpu.VMEM((128, lanes), F32),
-            pltpu.VMEM((64, 256), F32),
-            pltpu.VMEM((272, 256), F32),
-            pltpu.VMEM((144, 256), F32),
             pltpu.VMEM((144, 16), F32),
             pltpu.VMEM((128, lanes), F32),
             pltpu.VMEM((points, 256), BF16),
@@ -783,7 +791,10 @@
             pltpu.VMEM((4, 8, lanes), F32),
             pltpu.SemaphoreType.DMA((4,)),
             pltpu.SemaphoreType.DMA((4,)),
+            pltpu.SemaphoreType.DMA((4,)),
+            pltpu.SemaphoreType.DMA((7,)),
         ]
+        + [pltpu.VMEM(x.shape, x.dtype) for x in states[:5] + [levels, bins]]
         + sums,
         compiler_params=pltpu.CompilerParams(collective_id=0, has_side_effects=True, vmem_limit_bytes=LIMIT),
         name="step",

time: 113 us -> 110 us (0.973)
  Pallas kernels: 112 us -> 109 us
    pallas_call x1, Pallas kernels: 107 us -> 104 us  [per_device(): pl.pallas_call(functools.partial(step_kernel, sizes, groups, plans), out_...]
where the time goes in v4:
time: 110 us; the launch traced here: 109 us
  Pallas kernels  109 us (99%)
    pallas_call x1, Pallas kernels, per_device(): pl.pallas_call(functools.partial(step_kernel, sizes, groups, plans), out_...  104 us
    pallas_call x1, Pallas kernels, per_device(): pl.pallas_call(functools.partial(update_kernel, sizes['ty']), out_shape=[...  5.01 us

profile of v4, /device:TPU:0, one launch (start us, length us, event | category | flops | bytes accessed | tf_op | source)
XLA Modules:
  0.0 109.4 jit_solution(10704870329026629890)
XLA Ops:
  0.7 103.6 %step.1.grads = f32[1024,256]{1,0:T(8,128)} custom-call(s32[2,5]{1,0:T(2,128)} %bitcast.95, s32[16,16]{1,0:T(8,128)} %camera.1, s32[16,16]{1,0:T(8,128)} %ray_mask.1, f32[3,16,16]{2,1,0:T(8,128)} %direction.1, f32[3,16,16]{2,1,0:T(8,128)} %target.1, s32[256,128]{1,0:T(8,128)} %bitcast.85, s32[256,128]{1,0:T(8,128)} %bitcast.86, f32[3,100]{1,0:T(4,128)} %anchors.1, ...), custom_call_target="tpu_custom_call" | custom-call | tf_op jit(solution)/shard_map/step/pallas_call | solution.py:765
  104.3 5.0 %update.1 = (f32[1,1]{1,0:T(1,128)}, f32[1,64]{1,0:T(1,128)}, f32[63,2,256]{2,1,0:T(2,128)}, f32[2,256,256]{2,1,0:T(8,128)}, f32[283,2,128]{2,1,0:T(2,128)}, /*i...) custom-call(s32[2,5]{1,0:T(2,128)} %bitcast.96, ...), custom_call_target="tpu_custom_call" | custom-call | tf_op jit(solution)/shard_map/update/pallas_call | solution.py:803

commit v5 on v4

--- a/solution.py
+++ b/solution.py
@@ -280,7 +280,7 @@
     enc, h1, h2, hv, raw, depth, back, hist, w_e, w_mt, w_v, w_vt, w_c, w_ct, bias, per_ray,
     g_c, g_r, turned, mine, halo, send, recv, leaving, entering, *sums,
 ):
-    local, sums = sums[:7], sums[7:]
+    local, sums = sums[:13], sums[13:]
     tile_rows, tile_cols = camera.shape
     lanes = tile_rows * tile_cols
     cameras = anchors.shape[1]
@@ -303,13 +303,16 @@
     params, params_fine, counting = sum_of[:3]
     grads, grads_fine = sum_of[3:5], sum_of[5:7]
     expected = greet(groups, sides[:2])
-    given = (encoder, middle, viewer, colour, scalars, levels, bins)
+    given = (
+        owners, encoder, middle, viewer, colour, scalars,
+        camera, ray_mask, direction, target, anchors, levels, bins,
+    )
     inward = [pltpu.make_async_copy(x, here, entering.at[i]) for i, (x, here) in enumerate(zip(given, local))]
     for copy in inward:
         copy.start()
-    for copy in inward[:5]:
+    for copy in inward[:6]:
         copy.wait()
-    encoder, middle, viewer, colour, scalars, levels, bins = local
+    owners, encoder, middle, viewer, colour, scalars, camera, ray_mask, direction, target, anchors, levels, bins = local
 
     choose_e = selector(64, encoder.shape[0], LPOS, 32, BF16)
     choose_d = selector(32, viewer.shape[0] - 256, LDIR, 16, BF16)
@@ -319,6 +322,8 @@
     pl.semaphore_wait(pltpu.get_barrier_semaphore(), expected)
     params.step(0)
 
+    for copy in inward[6:]:
+        copy.wait()
     tall = jnp.concatenate(
         [direction[k] for k in range(3)]
         + [target[k] for k in range(3)]
@@ -366,8 +371,6 @@
     bottom = jnp.where(row16 >= 12, jnp.where(row16 == 12, 1.0, 0.0), cos_d)
     view_code = jnp.concatenate([top, bottom], 0).astype(BF16)
 
-    for copy in inward[5:]:
-        copy.wait()
     samples_fine = levels.shape[1]
     blocks_of = (SC // GROUP, samples_fine // GROUP)
     first_block = (0, blocks_of[0])
@@ -639,6 +642,8 @@
         lax.fori_loop(0, chunks, backward, 0)
         if net == 0:
             params_fine.step(params.steps - 1)
+        else:
+            grads_fine[0].step(0)
 
         tints = jnp.concatenate([g_c[...], jnp.zeros((144, 112), F32)], 1)
         tints, sums_c = tints[:128].T[:16], tints[128:136].T[:16, 0:1]
@@ -655,7 +660,8 @@
     for k in range(1, lanes // 128):
         fold = fold + loss[:, k * 128 : k * 128 + 128]
     rest[ROW_D - 223 : ROW_D - 222, 0:128] = fold
-    for k in range(params.steps):
+    grads_fine[1].step(0)
+    for k in range(1, params.steps):
         for part in grads_fine:
             part.step(k)
     outward = [
@@ -679,16 +685,31 @@
     return (weight_next, moment_next, square_next)
 
 
-def update_kernel(tiles_y, owners, grads, *refs):
-    given, loss, histogram, taken = refs[0:15], refs[15], refs[16], refs[17:32]
-    held, arrived, left = refs[32:47], refs[47], refs[48]
+def update_kernel(tiles_y, owners_given, grads_given, *refs):
+    given, outs, taken = refs[0:15], refs[15:17], refs[17:32]
+    held = refs[32:47]
+    grads, owners, loss, histogram, arrived, left, ends = refs[47:]
     device = lax.axis_index("tx") * tiles_y + lax.axis_index("ty")
     order = (1, 2, 0, 4, 3)
+    fetch = [
+        pltpu.make_async_copy(grads_given, grads, ends.at[0]),
+        pltpu.make_async_copy(owners_given, owners, ends.at[1]),
+    ]
+    for copy in fetch:
+        copy.start()
     for group in order:
         for i in (group, group + 5, group + 10):
             pltpu.make_async_copy(given[i], held[i], arrived.at[i]).start()
+    for copy in fetch:
+        copy.wait()
     histogram[...] = grads[ROWS + ROW_D + 32 : ROWS + ROW_D + 33, 0:NHIST]
     loss[...] = jnp.sum(grads[ROWS + ROW_D + 33 : ROWS + ROW_D + 34, 0:128], 1, keepdims=True)
+    figures = [
+        pltpu.make_async_copy(loss, outs[0], ends.at[2]),
+        pltpu.make_async_copy(histogram, outs[1], ends.at[3]),
+    ]
+    for copy in figures:
+        copy.start()
 
     def step(group, at, gradient):
         trio = (held[group], held[group + 5], held[group + 10])
@@ -734,6 +755,8 @@
             pltpu.make_async_copy(held[i], taken[i], left.at[i]).start()
     for i in range(15):
         pltpu.make_async_copy(held[i], taken[i], left.at[i]).wait()
+    for copy in figures:
+        copy.wait()
 
 
 ANY_SPEC = pl.BlockSpec(memory_space=pl.ANY)
@@ -762,10 +785,11 @@
     points = CHUNK * lanes
     chunks = samples // CHUNK
     blocks = samples // GROUP
+    small = [camera, ray_mask, ray_direction, target, anchors]
     grads = pl.pallas_call(
         functools.partial(step_kernel, sizes, groups, plans),
         out_shape=jax.ShapeDtypeStruct((2 * ROWS, 256), F32),
-        in_specs=[SMEM_SPEC] + [VMEM_SPEC] * 4 + [ANY_SPEC] * 2 + [VMEM_SPEC] + [ANY_SPEC] * 5,
+        in_specs=[ANY_SPEC] * 13,
         out_specs=ANY_SPEC,
         scratch_shapes=[
             pltpu.VMEM((blocks + SC // GROUP, 64, GROUP * lanes), BF16),
@@ -792,9 +816,10 @@
             pltpu.SemaphoreType.DMA((4,)),
             pltpu.SemaphoreType.DMA((4,)),
             pltpu.SemaphoreType.DMA((4,)),
-            pltpu.SemaphoreType.DMA((7,)),
+            pltpu.SemaphoreType.DMA((13,)),
+            pltpu.SMEM((2, 5), jnp.int32),
         ]
-        + [pltpu.VMEM(x.shape, x.dtype) for x in states[:5] + [levels, bins]]
+        + [pltpu.VMEM(x.shape, x.dtype) for x in states[:5] + small + [levels, bins]]
         + sums,
         compiler_params=pltpu.CompilerParams(collective_id=0, has_side_effects=True, vmem_limit_bytes=LIMIT),
         name="step",
@@ -804,10 +829,18 @@
         functools.partial(update_kernel, sizes["ty"]),
         out_shape=[jax.ShapeDtypeStruct((1, 1), F32), jax.ShapeDtypeStruct((1, NHIST), F32)]
         + [jax.ShapeDtypeStruct(x.shape, F32) for x in states],
-        in_specs=[SMEM_SPEC, VMEM_SPEC] + [ANY_SPEC] * 15,
-        out_specs=[VMEM_SPEC] * 2 + [ANY_SPEC] * 15,
+        in_specs=[ANY_SPEC] * 17,
+        out_specs=[ANY_SPEC] * 17,
         scratch_shapes=[pltpu.VMEM(x.shape, F32) for x in states]
-        + [pltpu.SemaphoreType.DMA((15,)), pltpu.SemaphoreType.DMA((15,))],
+        + [
+            pltpu.VMEM((2 * ROWS, 256), F32),
+            pltpu.SMEM((2, 5), jnp.int32),
+            pltpu.VMEM((1, 1), F32),
+            pltpu.VMEM((1, NHIST), F32),
+            pltpu.SemaphoreType.DMA((15,)),
+            pltpu.SemaphoreType.DMA((15,)),
+            pltpu.SemaphoreType.DMA((4,)),
+        ],
         name="update",
     )(owners.T, grads, *states)
     turned = []

time: 110 us -> 108 us (0.982)
  Pallas kernels: 109 us -> 107 us
where the time goes in v5:
time: 108 us
  Pallas kernels  107 us (99%)
    pallas_call x1, Pallas kernels, per_device(): pl.pallas_call(functools.partial(step_kernel, sizes, groups, plans), out_...  103 us
    pallas_call x1, Pallas kernels, per_device(): pl.pallas_call(functools.partial(update_kernel, sizes['ty']), out_shape=[...  4.12 us

profile of v5, /device:TPU:0, one launch (start us, length us, event | category | flops | bytes accessed | tf_op | source)
XLA Modules:
  0.0 107.6 jit_solution(14112147752944917375)
XLA Ops:
  0.7 102.6 %step.1.grads_given = f32[1024,256]{1,0:T(8,128)} custom-call(s32[2,5]{1,0:T(2,128)} %bitcast.95, s32[16,16]{1,0:T(8,128)} %camera.1, s32[16,16]{1,0:T(8,128)} %ray_mask.1, f32[3,16,16]{2,1,0:T(8,128)} %direction.1, f32[3,16,16]{2,1,0:T(8,128)} %target.1, s32[256,128]{1,0:T(8,128)} %bitcast.85, s32[256,128]{1,0:T(8,128)} %bitcast.86, f32[3,100]{1,0:T(4,128)} %anchors.1, ...), custom_call_target="tpu_custom_call" | custom-call | tf_op jit(solution)/shard_map/step/pallas_call | solution.py:789
  103.3 4.1 %update.1 = (f32[1,1]{1,0:T(1,128)}, f32[1,64]{1,0:T(1,128)}, f32[63,2,256]{2,1,0:T(2,128)}, f32[2,256,256]{2,1,0:T(8,128)}, f32[283,2,128]{2,1,0:T(2,128)}, /*i...) custom-call(s32[2,5]{1,0:T(2,128)} %bitcast.96, ...), custom_call_target="tpu_custom_call" | custom-call | tf_op jit(solution)/shard_map/update/pallas_call | solution.py:828

commit v6 on v5

--- a/solution.py
+++ b/solution.py
@@ -494,6 +494,14 @@
 
         lax.fori_loop(0, chunks, forward, 0)
 
+        upper, lower = [part.source for part in (grads, grads_fine)[net]]
+        g_m = upper
+        g_v, g_e = lower.at[ROW_V - 256 : ROW_V - 112], lower.at[ROW_E - 256 : ROW_E - 192]
+
+        def clear():
+            for ref in (upper, lower, g_c, g_r):
+                ref[...] = jnp.zeros_like(ref)
+
         before = jnp.zeros((1, lanes), F32)
         shade = [jnp.zeros((8, lanes), F32) for _ in range(3)]
         far, opaque = jnp.zeros((8, lanes), F32), jnp.zeros((8, lanes), F32)
@@ -527,7 +535,9 @@
         loss = loss + ray_weight * (miss[0] * miss[0] + miss[1] * miss[1] + miss[2] * miss[2])
         seed = [2.0 * ray_weight * miss[k] for k in range(3)]
         seed_depth = seed_opaque = None
-        if net == 1:
+        if net == 0:
+            clear()
+        else:
             for k in range(3):
                 mine[k : k + 1] = shade[k]
             mine[3:4] = far
@@ -541,6 +551,7 @@
 
             for i in range(4):
                 pl.when(sides[i][1])(lambda i=i: across(i, i).start())
+            clear()
 
             def count_bin(b, carry):
                 sums = jnp.zeros((8, lanes), F32)
@@ -606,12 +617,6 @@
             back[3, b] = dq * spacing(b) * jax.nn.sigmoid(raw[3, b] + sigma_bias)
             for k in range(3):
                 back[k, b] = w * seed[k] * tint[k] * (1.0 - tint[k])
-
-        upper, lower = [part.source for part in (grads, grads_fine)[net]]
-        g_m = upper
-        g_v, g_e = lower.at[ROW_V - 256 : ROW_V - 112], lower.at[ROW_E - 256 : ROW_E - 192]
-        for ref in (upper, lower, g_c, g_r):
-            ref[...] = jnp.zeros_like(ref)
 
         def backward(c, carry):
             send_on(net, "backward", c)
@@ -745,14 +750,19 @@
             bias = pltpu.roll(jnp.broadcast_to(bias, (8, 256)), 1, 1)[0:1]
             step(4, (spot, slice(768, 900)), (misc[2:3] + bias)[:, :132])
 
+    def send(group):
+        for i in (group, group + 5, group + 10):
+            pltpu.make_async_copy(held[i], taken[i], left.at[i]).start()
+
+    mine = [(owners[0, group] == device) | (owners[1, group] == device) for group in range(5)]
     for group in order:
-        trio = (group, group + 5, group + 10)
-        for i in trio:
+        for i in (group, group + 5, group + 10):
             pltpu.make_async_copy(given[i], held[i], arrived.at[i]).wait()
+        pl.when(jnp.logical_not(mine[group]))(functools.partial(send, group))
+    for group in order:
         for net in range(2):
             pl.when(owners[net, group] == device)(functools.partial(update, group, net))
-        for i in trio:
-            pltpu.make_async_copy(held[i], taken[i], left.at[i]).start()
+        pl.when(mine[group])(functools.partial(send, group))
     for i in range(15):
         pltpu.make_async_copy(held[i], taken[i], left.at[i]).wait()
     for copy in figures:

time: 108 us -> 108 us (level)
  no operation moved by 1% of the time
where the time goes in v6:
time: 108 us
  Pallas kernels  107 us (99%)
    pallas_call x1, Pallas kernels, per_device(): pl.pallas_call(functools.partial(step_kernel, sizes, groups, plans), out_...  103 us
    pallas_call x1, Pallas kernels, per_device(): pl.pallas_call(functools.partial(update_kernel, sizes['ty']), out_shape=[...  4.16 us

profile of v6, /device:TPU:0, one launch (start us, length us, event | category | flops | bytes accessed | tf_op | source)
XLA Modules:
  0.0 107.6 jit_solution(14944737032187386210)
XLA Ops:
  0.7 102.7 %step.1.grads_given = f32[1024,256]{1,0:T(8,128)} custom-call(s32[2,5]{1,0:T(2,128)} %bitcast.95, s32[16,16]{1,0:T(8,128)} %camera.1, s32[16,16]{1,0:T(8,128)} %ray_mask.1, f32[3,16,16]{2,1,0:T(8,128)} %direction.1, f32[3,16,16]{2,1,0:T(8,128)} %target.1, s32[256,128]{1,0:T(8,128)} %bitcast.85, s32[256,128]{1,0:T(8,128)} %bitcast.86, f32[3,100]{1,0:T(4,128)} %anchors.1, ...), custom_call_target="tpu_custom_call" | custom-call | tf_op jit(solution)/shard_map/step/pallas_call | solution.py:799
  103.3 4.2 %update.1 = (f32[1,1]{1,0:T(1,128)}, f32[1,64]{1,0:T(1,128)}, f32[63,2,256]{2,1,0:T(2,128)}, f32[2,256,256]{2,1,0:T(8,128)}, f32[283,2,128]{2,1,0:T(2,128)}, /*i...) custom-call(s32[2,5]{1,0:T(2,128)} %bitcast.96, ...), custom_call_target="tpu_custom_call" | custom-call | tf_op jit(solution)/shard_map/update/pallas_call | solution.py:838
